TPU v7x, 128 devices: a whole 4x4x4 slice. The times are simulated.
128 devices in a mesh: prow: 16 (over x, z_hi, core), pcol: 8 (over z_lo, y).
Axes of the slice: x: 4, y: 4, z: 4 (z_hi: 2, z_lo: 2; z = z_hi * 2 + z_lo), core: 2. Of those that a mesh axis runs over, the one named last changes fastest.
Arguments:
- inverse: bfloat16 [4, 8192, 8, 4096], P(None, 'prow', None, 'pcol'), may hold values from -6 to 6
- panel: bfloat16 [2, 4, 8192, 256], P(None, None, 'prow'), may hold values from -0.0625 to 0.0625
- structure: int32 [2, 16], replicated, may hold values from 0 to 63, as said below
- diag_inverse: float32 [2, 256, 256], replicated, may hold values from -6 to 6
Outputs:
- off_diag: bfloat16 [2, 4, 8192, 256], P(None, None, ('prow', 'pcol'))
- diag_block: float32 [2, 256, 256], replicated
Inputs may be any that keep to these rules, and one draw needn't show every extreme that they name: `structure`: each row lists 16 distinct block indices in increasing order, exactly one of them congruent to p modulo 16 for every p, and always includes the last ancestor block 63.
All inputs are finite; a program needn't handle non-finite values.
Results may differ from a plain program's by a relative error of at most 0.0022.
Values may be sent and summed in bfloat16 or wider, within the bound.
No kernel may reach another device: no remote copies, remote signals or barrier semaphores. Data moves between devices by JAX's collectives and lax.ppermute only.
A program may use at most 128 MiB of HBM per device.

v0:
```python
import jax
import jax.numpy as jnp
from jax import lax
from jax.sharding import PartitionSpec as P


def cut_along(array, dim, count):
    before, after = (array.shape[:dim], array.shape[dim + 1 :])
    return jnp.moveaxis(array.reshape(*before, count, -1, *after), dim, 0)


def sum_at_owner(array, axis, dim):
    tiles = cut_along(array, dim, lax.axis_size(axis))
    arrived = lax.all_to_all(tiles, axis, split_axis=0, concat_axis=0, tiled=True)
    return arrived.sum(axis=0)


def on_device(inverse, panel, structure, diag_inverse):
    prow_count = lax.axis_size("prow")
    pcol_count = lax.axis_size("pcol")
    prow_index = lax.axis_index("prow")
    pcol_index = lax.axis_index("pcol")
    rows_local, block_size, cols_local, _ = inverse.shape
    panel_width = panel.shape[3]
    total_blocks = rows_local * prow_count
    piece_rows = block_size // pcol_count
    owner_ratio = prow_count // pcol_count
    repeat_count = cols_local // owner_ratio
    positions = jnp.arange(total_blocks, dtype=jnp.int32)
    local_rows = jnp.arange(rows_local, dtype=jnp.int32)
    pieces = []
    products = []
    for supernode in range(structure.shape[0]):
        chosen = structure[supernode]
        selected = jnp.any(chosen[:, None] == positions[None, :], axis=0)
        own_rows = lax.dynamic_index_in_dim(
            selected.reshape(rows_local, prow_count), prow_index, 1, keepdims=False
        )
        own_cols = lax.dynamic_index_in_dim(
            selected.reshape(cols_local, pcol_count), pcol_index, 1, keepdims=False
        )
        local_panel = panel[supernode]
        row_pick = jnp.sum(jnp.where(own_rows, local_rows, 0))
        single = lax.dynamic_index_in_dim(local_panel, row_pick, 0, keepdims=False)
        gathered = lax.all_gather(single, "prow", axis=0, tiled=True)
        gathered = gathered.reshape(owner_ratio, pcol_count, block_size, panel_width)
        owner_blocks = lax.dynamic_index_in_dim(gathered, pcol_index, 1, keepdims=False)
        tiled = jnp.broadcast_to(
            owner_blocks[None], (repeat_count, owner_ratio, block_size, panel_width)
        )
        tiled = tiled.reshape(cols_local, block_size, panel_width)
        column_panel = tiled * own_cols.astype(jnp.bfloat16)[:, None, None]
        ranking = jnp.where(own_cols, 0, cols_local) + jnp.arange(cols_local, dtype=jnp.int32)
        column_order = jnp.argsort(ranking)
        live_count = jnp.sum(own_cols.astype(jnp.int32))

        def add_column(position_index, running):
            column = column_order[position_index]
            block_column = lax.dynamic_index_in_dim(inverse, column, 2, keepdims=False)
            factor = lax.dynamic_index_in_dim(column_panel, column, 0, keepdims=False)
            return running + jnp.einsum(
                "rab,bw->raw", block_column, factor, preferred_element_type=jnp.float32
            )

        starting = jnp.zeros((rows_local, block_size, panel_width), jnp.float32)
        partial_value = lax.fori_loop(0, live_count, add_column, starting)
        partial_value = -partial_value * own_rows.astype(jnp.float32)[:, None, None]
        summed = sum_at_owner(partial_value, "pcol", 1)
        rounded = summed.astype(jnp.bfloat16)
        pieces.append(rounded)
        factor_rows = lax.dynamic_slice_in_dim(local_panel, pcol_index * piece_rows, piece_rows, 1)
        products.append(
            jnp.einsum("raw,rav->wv", factor_rows, rounded, preferred_element_type=jnp.float32)
        )
    diagonal_terms = lax.psum(jnp.stack(products), ("prow", "pcol"))
    return (jnp.stack(pieces), diag_inverse - diagonal_terms)


def solution(mesh):
    placed = (P(None, "prow", None, "pcol"), P(None, None, "prow", None), P(), P())
    return jax.shard_map(
        on_device,
        mesh=mesh,
        in_specs=placed,
        out_specs=(P(None, None, ("prow", "pcol"), None), P()),
        check_vma=False,
    )
```

profile of v0, /device:TPU:1, one launch (start us, length us, event | category | flops | bytes accessed | tf_op | source)
XLA Modules:
  0.0 347.8 jit_solution(9517647593599522379)
XLA Ops:
  10.6 1.7 fusion.30
  16.7 16.7 %copy.16 = bf16[4,512,8,512]{3,1,0,2:T(8,128)(2,1)} copy(bf16[4,512,8,512]{3,2,1,0:T(8,128)(2,1)} %param.8) | data formatting | bytes 33554432 | tf_op jit(solution)/shard_map/while | solution.py:66
  36.1 37.5 %all-gather.5.cloned.1.call-done = bf16[1,1,8192,256]{3,2,1,0:T(8,128)(2,1)} async-done(((bf16[1,1,512,256]{3,2,1,0:T(8,128)(2,1)}), bf16[1,1,8192,256]{3,2,1,0:T(8,128)(2,1)}) %all-gather.5.cloned.1.call-update) | async-done | bytes 4194320 | tf_op jit(solution)/shard_map/all_gather | solution.py:45
  73.6 1.1 dynamic-slice_bitcast_fusion.1
  74.7 1.6 bitcast_multiply_fusion.1
  76.4 11.7 %while.20 = (s32[]{:T(128)}, f32[4,512,256]{2,1,0:T(8,128)S(1)}, s32[]{:T(128)}, s32[8]{0:T(128)S(1)}, bf16[4,512,8,512]{3,1,0,2:T(8,128)(2,1)}, /*index=5*/bf16...) while((s32[]{:T(128)}, f32[4,512,256]{2,1,0:T(8,128)S(1)}, s32[]{:T(128)}, s32[8]{0:T(128)S(1)}, ...), condition=%wide.region_5.6_spmd, body=%wide.region_4.5_spmd.sunk | while | flops 537395200 | bytes 6554797 | solution.py:66
  79.6 2.3 fusion.41
  85.1 2.4 fusion.41
  88.4 1.5 copy.17
  89.9 4.3 %all-to-all-start = ((f32[8,4,64,256]{3,2,1,0:T(8,128)}), f32[8,4,64,256]{3,2,1,0:T(8,128)}, u32[]{:S(2)}, u32[]{:S(2)}) async-start(f32[8,4,64,256]{3,2,1,0:T(8,128)} %copy.17), calls=%async_computation | async-start | bytes 4194304 | tf_op jit(solution)/shard_map/all_to_all | solution.py:14
  95.5 45.2 %all-gather.7.cloned.1.call-done = bf16[1,1,8192,256]{3,2,1,0:T(8,128)(2,1)} async-done(((bf16[1,1,512,256]{3,2,1,0:T(8,128)(2,1)}), bf16[1,1,8192,256]{3,2,1,0:T(8,128)(2,1)}) %all-gather.7.cloned.1.call-update) | async-done | bytes 4194320 | tf_op jit(solution)/shard_map/all_gather | solution.py:45
  140.7 1.1 dynamic-slice_bitcast_fusion
  141.7 1.6 bitcast_multiply_fusion
  143.5 11.8 %while.21 = (s32[]{:T(128)}, f32[4,512,256]{2,1,0:T(8,128)S(1)}, s32[]{:T(128)}, s32[8]{0:T(128)S(1)}, bf16[4,512,8,512]{3,1,0,2:T(8,128)(2,1)}, /*index=5*/bf16...) while((s32[]{:T(128)}, f32[4,512,256]{2,1,0:T(8,128)S(1)}, s32[]{:T(128)}, s32[8]{0:T(128)S(1)}, ...), condition=%wide.region_12.13_spmd, body=%wide.region_11.12_spmd.sunk | while | flops 537395200 | bytes 6554797 | solution.py:66
  146.7 2.3 fusion.44
  152.3 2.3 fusion.44
  155.6 1.5 copy.19
  157.1 4.3 %all-to-all-start.1 = ((f32[8,4,64,256]{3,2,1,0:T(8,128)}), f32[8,4,64,256]{3,2,1,0:T(8,128)S(1)}, u32[]{:S(2)}, u32[]{:S(2)}) async-start(f32[8,4,64,256]{3,2,1,0:T(8,128)} %copy.19), calls=%async_computation.1 | async-start | bytes 4194304 | tf_op jit(solution)/shard_map/all_to_all | solution.py:14
  161.4 1.7 reduce_sum.56
  163.1 1.8 convolution_bitcast_fusion.1
  165.0 23.5 %all-to-all-done.1 = f32[8,4,64,256]{3,2,1,0:T(8,128)S(1)} async-done(((f32[8,4,64,256]{3,2,1,0:T(8,128)}), f32[8,4,64,256]{3,2,1,0:T(8,128)S(1)}, u32[]{:S(2)}, u32[]{:S(2)}) %all-to-all-start.1) | async-done | bytes 2097184 | tf_op jit(solution)/shard_map/all_to_all | solution.py:14
  188.8 1.8 pad_maximum_fusion
  191.4 148.0 %all-reduce.2.cloned.1.call-done = f32[2,256,256]{2,1,0:T(8,128)} async-done(((f32[2,256,256]{2,1,0:T(8,128)}), f32[2,256,256]{2,1,0:T(8,128)}) %all-reduce.2.cloned.1.call-update) | async-done | bytes 524304 | tf_op jit(solution)/shard_map/psum | solution.py:75
  339.4 1.9 sub.3
  (46 shorter events, 12.2 us)
Async XLA Ops:
  7.2 66.4 %all-gather.5.cloned.1.call-start = ((), (), s32[]{:S(2)}) async-start(), calls=%async_computation.3 | async-start | bytes 4456448 | tf_op jit(solution)/shard_map/all_gather | solution.py:45
  12.3 21.0 %copy-start = (bf16[1,4,512,256]{3,2,1,0:T(8,128)(2,1)}, bf16[1,4,512,256]{3,2,1,0:T(8,128)(2,1)S(1)}, u32[]{:S(2)}) copy-start(bf16[1,4,512,256]{3,2,1,0:T(8,128)(2,1)S(1)} %get-tuple-element.162) | copy-start | bytes 3145732
  13.7 126.9 %all-gather.7.cloned.1.call-start = ((), (), s32[]{:S(2)}) async-start(), calls=%async_computation.4 | async-start | bytes 4456448 | tf_op jit(solution)/shard_map/all_gather | solution.py:45
  89.9 67.2 %all-to-all-start = ((f32[8,4,64,256]{3,2,1,0:T(8,128)}), f32[8,4,64,256]{3,2,1,0:T(8,128)}, u32[]{:S(2)}, u32[]{:S(2)}) async-start(f32[8,4,64,256]{3,2,1,0:T(8,128)} %copy.17), calls=%async_computation | async-start | bytes 4194304 | tf_op jit(solution)/shard_map/all_to_all | solution.py:14
  157.1 31.4 %all-to-all-start.1 = ((f32[8,4,64,256]{3,2,1,0:T(8,128)}), f32[8,4,64,256]{3,2,1,0:T(8,128)S(1)}, u32[]{:S(2)}, u32[]{:S(2)}) async-start(f32[8,4,64,256]{3,2,1,0:T(8,128)} %copy.19), calls=%async_computation.1 | async-start | bytes 4194304 | tf_op jit(solution)/shard_map/all_to_all | solution.py:14
  161.4 178.0 %all-reduce.2.cloned.1.call-start = ((), (), s32[]{:S(2)}) async-start(), calls=%async_computation.2 | async-start | bytes 1048576 | tf_op jit(solution)/shard_map/psum | solution.py:75
  188.6 150.8 %copy-start.1 = (f32[2,256,256]{2,1,0:T(8,128)S(1)}, f32[2,256,256]{2,1,0:T(8,128)}, u32[]{:S(2)}) copy-start(f32[2,256,256]{2,1,0:T(8,128)} %param.11) | copy-start | bytes 1572868
Sparse Core Ops, SparseCore 0:
  13.9 59.6 all-gather.4
  76.6 64.0 all-gather.6
  190.8 148.5 all-reduce.1
where the time goes:
time: 349 us; the launch traced here: 348 us
  waiting for transfers between devices  254 us (73%)
  local copies, waits for them, and re-layouts  29.1 us (8%)
  between operations  17.8 us (5%)
  other arithmetic  14.8 us (4%)
  loops' own time  11.8 us (3%)
  matrix products  11.4 us (3%)
  starting transfers between devices  8.73 us (3%)
    psum x1, waiting for transfers between devices, on_device(): diagonal_terms = lax.psum(jnp.stack(products), ('prow', 'pcol'))  148 us
    all_gather x2, waiting for transfers between devices, on_device(): gathered = lax.all_gather(single, 'prow', axis=0, tiled=True)  82.7 us
    all_to_all x2, waiting for transfers between devices, sum_at_owner(): lax.all_to_all(tiles, axis, split_axis=0, concat_axis=0, tiled=True)  23.5 us
    while x1, local copies, waits for them, and re-layouts, on_device(): partial_value = lax.fori_loop(0, live_count, add_column, starting)  16.7 us
    another operation x2, loops' own time, on_device(): partial_value = lax.fori_loop(0, live_count, add_column, starting)  11.8 us
    dot_general x4, matrix products, add_column(): jnp.einsum('rab,bw->raw', block_column, factor, preferred_element_type=jn...  9.32 us
    all_to_all x2, starting transfers between devices, sum_at_owner(): lax.all_to_all(tiles, axis, split_axis=0, concat_axis=0, tiled=True)  8.61 us
  transfers between devices with their start and end apart: 5, of which 4 were waited for; matrix products, arithmetic and copies ran while one was open for 13% of the time, Pallas kernels for 0%

commit v1 on v0

v1 whole, which is shorter than its diff:
```python
import functools

import jax
import jax.numpy as jnp
from jax import lax
from jax.experimental import pallas as pl
from jax.experimental.pallas import tpu as pltpu
from jax.sharding import PartitionSpec as P

BOTH = ("prow", "pcol")
SMEM = pl.BlockSpec(memory_space=pltpu.SMEM)
VMEM = pl.BlockSpec(memory_space=pltpu.VMEM)
ANY = pl.BlockSpec(memory_space=pl.ANY)
HBM = pl.BlockSpec(memory_space=pltpu.HBM)
VMEM_LIMIT = 48 * 1024 * 1024
SHIFT = (2, 0, 1, 3)


def spread():
    pairs = []
    for row in range(16):
        x, z_hi, core = row // 4, row // 2 % 2, row % 2
        for col in range(8):
            z_lo, y = col // 4, col % 4
            to_x = (x + SHIFT[(y - (z_hi * 2 + core)) % 4]) % 4
            to_z_hi = z_hi if z_lo == x % 2 else 1 - z_hi
            to_row = (to_x * 2 + to_z_hi) * 2 + x // 2
            pairs.append((row * 8 + col, to_row * 8 + row % 8))
    return pairs


SPREAD = spread()
SWAP = [(row, row ^ 1) for row in range(16)]
SAME_CORE = [[row for row in range(16) if row % 2 == core] for core in range(2)]


def pick_blocks(structure, panel, picks, chosen, sems):
    row, col = lax.axis_index("prow"), lax.axis_index("pcol")
    core = row & 1
    wanted = (row, col + 8 * core, col + 8 * (1 - core))
    copies = []
    for s in range(2):
        found = [jnp.int32(0)] * 3
        for k in range(16):
            entry = structure[s, k]
            for i in range(3):
                found[i] += jnp.where((entry & 15) == wanted[i], entry >> 4, 0)
        copies.append(pltpu.make_async_copy(panel.at[s, found[0]], chosen.at[s], sems.at[s]))
        copies[-1].start()
        picks[s, 0] = found[0]
        picks[s, 1] = 2 * found[1] + core
        picks[s, 2] = 2 * found[2] + 1 - core
    for copy in copies:
        copy.wait()


def extract(picks, block, out, wide):
    s = pl.program_id(0)
    rows = block.shape[1]
    for k in range(4):
        lanes = slice(128 * k, 128 * k + 128)
        wide[k] = block[0, :, :, lanes].astype(jnp.float32).reshape(rows * 8, 128)
        for i in range(2):
            column = wide[k, pl.ds(picks[s, 1 + i], rows, stride=8), :]
            out[0, i, :, lanes] = column.astype(jnp.bfloat16)


def multiply(blocks, own, other, out):
    for s in range(2):
        total = None
        for i, factor in enumerate((own, other)):
            term = lax.dot_general(
                factor[s], blocks[s, i], (((0,), (1,)), ((), ())), preferred_element_type=jnp.float32
            )
            total = term if total is None else total + term
        out[:, s] = (-total).reshape(8, 32, 512)


def round_and_project(arrived, chosen, columns, kept, sent):
    core = lax.axis_index("prow") & 1
    for s in range(2):
        total = arrived[0, s]
        for i in range(1, 8):
            total += arrived[i, s]
        rounded = total.astype(jnp.bfloat16)
        columns[s] = rounded
        term = jnp.dot(rounded, chosen[s], preferred_element_type=jnp.float32)
        first = core == 0
        kept[s] = jnp.where(first, term[:16], term[16:])
        sent[s] = jnp.where(first, term[16:], term[:16])


def pair_sum(kept, arrived, out):
    total = kept[...] + arrived[...]
    for i in range(8):
        out[i] = total


def pack(arrived, columns, out):
    for s in range(2):
        total = arrived[0, s]
        for i in range(1, 8):
            total += arrived[i, s]
        high = total.astype(jnp.bfloat16)
        low = (total - high.astype(jnp.float32)).astype(jnp.bfloat16)
        for i in range(8):
            out[i, 32 * s : 32 * s + 16] = high
            out[i, 32 * s + 16 : 32 * s + 32] = low
            out[i, 64:, 128 * s : 128 * s + 128] = columns[s, :, i // 2 * 128 : i // 2 * 128 + 128]


def finish(picks, own, other, diag_inverse, off_diag, diag_block):
    core = lax.axis_index("prow") & 1
    half = lax.axis_index("pcol") & 1
    off_diag[...] = jnp.zeros_like(off_diag)
    for s in range(2):
        slabs = []
        for i in range(8):
            high, low = (slice(32 * s + 16 * k, 32 * s + 16 * k + 16) for k in range(2))
            mine = own[i, high].astype(jnp.float32) + own[i, low].astype(jnp.float32)
            theirs = other[i, high].astype(jnp.float32) + other[i, low].astype(jnp.float32)
            slabs.append(jnp.where(core == 0, mine, theirs))
            slabs.append(jnp.where(core == 0, theirs, mine))
        diag_block[s] = diag_inverse[s] - jnp.concatenate(slabs, axis=0).T
        part = jnp.concatenate(
            [own[i, 64:, 128 * s : 128 * s + 128].astype(jnp.float32) for i in range(8)], axis=0
        ).T
        rows = jnp.where(half == 0, part[:64], part[64:])
        off_diag[s, picks[s, 0]] = rows.astype(jnp.bfloat16)


def call(body, out_shape, **rest):
    return pl.pallas_call(
        body,
        out_shape=out_shape,
        compiler_params=pltpu.CompilerParams(vmem_limit_bytes=VMEM_LIMIT),
        **rest,
    )


def on_device(inverse, panel, structure, diag_inverse):
    f32, bf16 = jnp.float32, jnp.bfloat16
    shape = jax.ShapeDtypeStruct
    picks, chosen = call(
        pick_blocks,
        (shape((2, 3), jnp.int32), shape((2, 512, 256), bf16)),
        in_specs=[SMEM, HBM],
        out_specs=(SMEM, ANY),
        scratch_shapes=[pltpu.SemaphoreType.DMA((2,))],
    )(structure, panel)
    own = lax.ppermute(chosen, BOTH, SPREAD)
    rows = 128
    blocks = call(
        extract,
        shape((2, 2, 512, 512), bf16),
        grid_spec=pltpu.PrefetchScalarGridSpec(
            num_scalar_prefetch=1,
            grid=(2, 512 // rows),
            in_specs=[pl.BlockSpec((1, rows, 8, 512), lambda s, i, picks: (picks[s, 0], i, 0, 0))],
            out_specs=pl.BlockSpec((1, 2, rows, 512), lambda s, i, picks: (s, 0, i, 0)),
            scratch_shapes=[pltpu.VMEM((4, rows * 8, 128), f32)],
        ),
        cost_estimate=pl.CostEstimate(flops=0, bytes_accessed=10 << 20, transcendentals=0),
    )(picks, inverse)
    own, blocks = lax.optimization_barrier((own, blocks))
    other = lax.ppermute(own, "prow", SWAP)
    partial = call(
        multiply,
        shape((8, 2, 32, 512), f32),
        in_specs=[VMEM, VMEM, VMEM],
        out_specs=VMEM,
    )(blocks, own, other)
    arrived = lax.all_to_all(partial, "pcol", 0, 0)
    columns, kept, sent = call(
        round_and_project,
        (shape((2, 32, 512), bf16), shape((2, 16, 256), f32), shape((2, 16, 256), f32)),
        in_specs=[VMEM, VMEM],
        out_specs=(VMEM, VMEM, VMEM),
    )(arrived, chosen)
    copies = call(
        pair_sum, shape((8, 2, 16, 256), f32), in_specs=[VMEM, VMEM], out_specs=VMEM
    )(kept, lax.ppermute(sent, "prow", SWAP))
    sums = lax.all_to_all(copies, "prow", 0, 0, axis_index_groups=SAME_CORE)
    packed = call(
        pack, shape((8, 96, 256), bf16), in_specs=[VMEM, VMEM], out_specs=VMEM
    )(sums, columns)
    final = lax.all_to_all(packed, "pcol", 0, 0)
    sibling = lax.ppermute(final[:, :64], "prow", SWAP)
    return call(
        finish,
        (shape((2, 4, 64, 256), bf16), shape((2, 256, 256), f32)),
        in_specs=[SMEM, VMEM, VMEM, VMEM],
        out_specs=(VMEM, VMEM),
    )(picks, final, sibling, diag_inverse)


def solution(mesh):
    placed = (P(None, "prow", None, "pcol"), P(None, None, "prow", None), P(), P())
    return jax.shard_map(
        on_device,
        mesh=mesh,
        in_specs=placed,
        out_specs=(P(None, None, ("prow", "pcol"), None), P()),
        check_vma=False,
    )
```

time: 349 us -> 77.1 us (0.22)
  waiting for transfers between devices: 254 us -> 4.76 us
  blocking collectives: 0 us -> 48.7 us
  local copies, waits for them, and re-layouts: 29.1 us -> 2.28 us
  between operations: 17.8 us -> 0.69 us
  other arithmetic: 14.8 us -> 0 us
  loops' own time: 11.8 us -> 0 us
  matrix products: 11.4 us -> 0 us
  Pallas kernels: 0 us -> 11.4 us
    psum x1 -> x0, waiting for transfers between devices: 148 us -> none  [on_device(): diagonal_terms = lax.psum(jnp.stack(products), ('prow', 'pcol'))]
    all_gather x2 -> x0, waiting for transfers between devices: 82.7 us -> none  [on_device(): gathered = lax.all_gather(single, 'prow', axis=0, tiled=True)]
    all_to_all x0 -> x3, blocking collectives: none -> 48.7 us  [the longest x1 25.5 us: on_device(): arrived = lax.all_to_all(partial, 'pcol', 0, 0)]
    all_to_all x2 -> x0, waiting for transfers between devices: 23.5 us -> none  [sum_at_owner(): lax.all_to_all(tiles, axis, split_axis=0, concat_axis=0, tiled=True)]
    while x1 -> x0, local copies, waits for them, and re-layouts: 16.7 us -> none  [on_device(): partial_value = lax.fori_loop(0, live_count, add_column, starting)]
    another operation x2 -> x0, loops' own time: 11.8 us -> none  [on_device(): partial_value = lax.fori_loop(0, live_count, add_column, starting)]
    pallas_call x0 -> x7, Pallas kernels: none -> 11.4 us  [the longest x1 7.42 us: on_device(): call(extract, shape((2, 2, 512, 512), bf16), grid_spec=pltpu.PrefetchScal...]
    dot_general x6 -> x0, matrix products: 11.4 us -> none  [the longest x4 9.32 us: add_column(): jnp.einsum('rab,bw->raw', block_column, factor, preferred_element_type=jn...]
  transfers between devices with their start and end apart: 5 -> 4, of which waited for: 4 -> 4; matrix products, arithmetic and copies ran while one was open for 13% -> 0% of each run, Pallas kernels for 0% -> 10%
where the time goes in v1:
time: 77.1 us; the launch traced here: 76.7 us
  blocking collectives  48.7 us (63%)
  Pallas kernels  11.4 us (15%)
  starting transfers between devices  8.75 us (11%)
  waiting for transfers between devices  4.76 us (6%)
  local copies, waits for them, and re-layouts  2.28 us (3%)
    all_to_all x1, blocking collectives, on_device(): arrived = lax.all_to_all(partial, 'pcol', 0, 0)  25.5 us
    all_to_all x1, blocking collectives, on_device(): sums = lax.all_to_all(copies, 'prow', 0, 0, axis_index_groups=SAME_CORE)  13.8 us
    all_to_all x1, blocking collectives, on_device(): final = lax.all_to_all(packed, 'pcol', 0, 0)  9.53 us
    pallas_call x1, Pallas kernels, on_device(): call(extract, shape((2, 2, 512, 512), bf16), grid_spec=pltpu.PrefetchScal...  7.42 us
    ppermute x1, starting transfers between devices, on_device(): own = lax.ppermute(chosen, BOTH, SPREAD)  4.96 us
    ppermute x1, starting transfers between devices, on_device(): sibling = lax.ppermute(final[:, :64], 'prow', SWAP)  2.9 us
    unnamed x6, local copies, waits for them, and re-layouts  2.27 us
    ppermute x1, waiting for transfers between devices, on_device(): other = lax.ppermute(own, 'prow', SWAP)  1.91 us
  transfers between devices with their start and end apart: 4, of which 4 were waited for; matrix products, arithmetic and copies ran while one was open for 0% of the time, Pallas kernels for 10%

profile of v1, /device:TPU:1, one launch (start us, length us, event | category | flops | bytes accessed | tf_op | source)
XLA Modules:
  0.0 76.7 jit_solution(11744886076666161785)
XLA Ops:
  0.6 0.0 copy-start
  0.6 1.6 %copy-done = bf16[2,4,512,256]{3,2,1,0:T(8,128)(2,1)S(1)} copy-done((bf16[2,4,512,256]{3,2,1,0:T(8,128)(2,1)S(1)}, bf16[2,4,512,256]{3,2,1,0:T(8,128)(2,1)}, u32[]{:S(2)}) %copy-start) | copy-done | bytes 2097176
  2.2 0.0 copy-start.2
  2.2 0.7 copy-done.2
  2.9 1.3 %shard_map.59 = (s32[2,3]{1,0:T(2,128)S(1)}, bf16[2,512,256]{2,1,0:T(8,128)(2,1)S(1)}) custom-call(s32[2,16]{1,0:T(2,128)S(1)} %copy-done.2, bf16[2,4,512,256]{3,2,1,0:T(8,128)(2,1)S(1)} %copy-done), custom_call_target="tpu_custom_call" | custom-call | tf_op jit(solution)/shard_map/pallas_call | solution.py:144
  4.3 5.0 %collective-permute-start = (bf16[2,512,256]{2,1,0:T(8,128)(2,1)S(1)}, bf16[2,512,256]{2,1,0:T(8,128)(2,1)S(1)}, u32[]{:S(2)}, u32[]{:S(2)}) collective-permute-start(bf16[2,512,256]{2,1,0:T(8,128)(2,1)S(1)} %get-tuple-element.10.chosen), channel_id=1, source_target_pairs={{0,64},{1,0},{2,32},{3,96},{4,80},{5,16},{6,48},{7,112},{8,97},{9,... | collective-permute-start | bytes 1572872 | tf_op jit(solution)/shard_map/ppermute | solution.py:151
  9.2 7.4 %shard_map.60.blocks = bf16[2,2,512,512]{3,2,1,0:T(8,128)(2,1)S(1)} custom-call(s32[2,3]{1,0:T(2,128)S(1)} %get-tuple-element.9.picks, bf16[4,512,8,512]{3,2,1,0:T(8,128)(2,1)} %block.1), custom_call_target="tpu_custom_call" | custom-call | bytes 10485760 | tf_op jit(solution)/shard_map/pallas_call | solution.py:153
  16.6 0.8 %collective-permute-done.own = bf16[2,512,256]{2,1,0:T(8,128)(2,1)S(1)} collective-permute-done((bf16[2,512,256]{2,1,0:T(8,128)(2,1)S(1)}, bf16[2,512,256]{2,1,0:T(8,128)(2,1)S(1)}, u32[]{:S(2)}, u32[]{:S(2)}) %collective-permute-start) | collective-permute-done | bytes 524320 | tf_op jit(solution)/shard_map/ppermute | solution.py:151
  17.5 0.0 collective-permute-start.1
  17.5 1.9 %collective-permute-done.1.other = bf16[2,512,256]{2,1,0:T(8,128)(2,1)S(1)} collective-permute-done((bf16[2,512,256]{2,1,0:T(8,128)(2,1)S(1)}, bf16[2,512,256]{2,1,0:T(8,128)(2,1)S(1)}, u32[]{:S(2)}, u32[]{:S(2)}) %collective-permute-start.1) | collective-permute-done | bytes 524320 | tf_op jit(solution)/shard_map/ppermute | solution.py:166
  19.4 0.7 shard_map.61
  20.1 25.5 %all_to_all.15.arrived = f32[8,2,32,512]{3,2,1,0:T(8,128)S(1)} all-to-all(f32[8,2,32,512]{3,2,1,0:T(8,128)S(1)} %shard_map.61), channel_id=1, replica_groups=mesh['prow'=16,'pcol'=8] {'pcol'}, dimensions={0} | all-to-all | bytes 2097152 | tf_op jit(solution)/shard_map/all_to_all | solution.py:173
  45.6 0.0 copy-start.1
  45.6 0.2 shard_map.62
  45.8 0.9 %collective-permute-start.2 = (f32[2,16,256]{2,1,0:T(8,128)S(1)}, f32[2,16,256]{2,1,0:T(8,128)S(1)}, u32[]{:S(2)}, u32[]{:S(2)}) collective-permute-start(f32[2,16,256]{2,1,0:T(8,128)S(1)} %get-tuple-element.14), channel_id=1, source_target_pairs={{0,8},{8,0},{16,24},{24,16},{32,40},{40,32},{48,56},{56,48},{64,72... | collective-permute-start | bytes 98312 | tf_op jit(solution)/shard_map/ppermute | solution.py:182
  46.7 0.9 %collective-permute-done.2.arrived = f32[2,16,256]{2,1,0:T(8,128)S(1)} collective-permute-done((f32[2,16,256]{2,1,0:T(8,128)S(1)}, f32[2,16,256]{2,1,0:T(8,128)S(1)}, u32[]{:S(2)}, u32[]{:S(2)}) %collective-permute-start.2) | collective-permute-done | bytes 32800 | tf_op jit(solution)/shard_map/ppermute | solution.py:182
  47.6 13.8 %all_to_all.16.arrived = f32[8,2,16,256]{3,2,1,0:T(8,128)S(1)} all-to-all(f32[8,2,16,256]{3,2,1,0:T(8,128)S(1)} %shard_map.63), channel_id=1, replica_groups={{0,16,32,48,64,80,96,112},{8,24,40,56,72,88,104,120},{1,17,33,49,65,81,..., dimensions={0} | all-to-all | bytes 524288 | tf_op jit(solution)/shard_map/all_to_all | solution.py:183
  61.4 9.5 %all_to_all.17.own = bf16[8,96,256]{2,1,0:T(8,128)(2,1)S(1)} all-to-all(bf16[8,96,256]{2,1,0:T(8,128)(2,1)S(1)} %shard_map.64), channel_id=1, replica_groups=mesh['prow'=16,'pcol'=8] {'pcol'}, dimensions={0} | all-to-all | bytes 786432 | tf_op jit(solution)/shard_map/all_to_all | solution.py:187
  70.9 2.9 %collective-permute-start.3 = (bf16[8,64,256]{2,1,0:T(8,128)(2,1)S(1)}, bf16[8,64,256]{2,1,0:T(8,128)(2,1)S(1)}, u32[]{:S(2)}, u32[]{:S(2)}) collective-permute-start(bf16[8,64,256]{2,1,0:T(8,128)(2,1)S(1)} %slice.4), channel_id=1, source_target_pairs={{0,8},{8,0},{16,24},{24,16},{32,40},{40,32},{48,56},{56,48},{64,72... | collective-permute-start | bytes 786440 | tf_op jit(solution)/shard_map/ppermute | solution.py:188
  73.8 1.2 %collective-permute-done.3.other = bf16[8,64,256]{2,1,0:T(8,128)(2,1)S(1)} collective-permute-done((bf16[8,64,256]{2,1,0:T(8,128)(2,1)S(1)}, bf16[8,64,256]{2,1,0:T(8,128)(2,1)S(1)}, u32[]{:S(2)}, u32[]{:S(2)}) %collective-permute-start.3) | collective-permute-done | bytes 262176 | tf_op jit(solution)/shard_map/ppermute | solution.py:188
  75.0 0.0 copy-done.1
  75.0 1.7 %shard_map.65 = (bf16[2,4,64,256]{3,2,1,0:T(8,128)(2,1)}, f32[2,256,256]{2,1,0:T(8,128)}) custom-call(s32[2,3]{1,0:T(2,128)S(1)} %get-tuple-element.9.picks, bf16[8,96,256]{2,1,0:T(8,128)(2,1)S(1)} %all_to_all.17.own, bf16[8,64,256]{2,1,0:T(8,128)(2,1)S(1)} %collective-permute-done.3.other, f32[2,256,256]{2,1,0:T(8,128)S(1)} %copy-done.1), custom_call_target="tpu_custom_call" | custom-call | tf_op jit(solution)/shard_map/pallas_call | solution.py:189
  (3 shorter events, 0.1 us)
Async XLA Ops:
  0.6 1.6 %copy-start = (bf16[2,4,512,256]{3,2,1,0:T(8,128)(2,1)S(1)}, bf16[2,4,512,256]{3,2,1,0:T(8,128)(2,1)}, u32[]{:S(2)}) copy-start(bf16[2,4,512,256]{3,2,1,0:T(8,128)(2,1)} %panel.1) | copy-start | bytes 6291460
  2.2 0.7 copy-start.2
  4.3 13.2 %collective-permute-start = (bf16[2,512,256]{2,1,0:T(8,128)(2,1)S(1)}, bf16[2,512,256]{2,1,0:T(8,128)(2,1)S(1)}, u32[]{:S(2)}, u32[]{:S(2)}) collective-permute-start(bf16[2,512,256]{2,1,0:T(8,128)(2,1)S(1)} %get-tuple-element.10.chosen), channel_id=1, source_target_pairs={{0,64},{1,0},{2,32},{3,96},{4,80},{5,16},{6,48},{7,112},{8,97},{9,... | collective-permute-start | bytes 1572872 | tf_op jit(solution)/shard_map/ppermute | solution.py:151
  17.5 1.9 %collective-permute-start.1 = (bf16[2,512,256]{2,1,0:T(8,128)(2,1)S(1)}, bf16[2,512,256]{2,1,0:T(8,128)(2,1)S(1)}, u32[]{:S(2)}, u32[]{:S(2)}) collective-permute-start(bf16[2,512,256]{2,1,0:T(8,128)(2,1)S(1)} %collective-permute-done.own), channel_id=1, source_target_pairs={{0,8},{8,0},{16,24},{24,16},{32,40},{40,32},{48,56},{56,48},{64,72... | collective-permute-start | bytes 1572872 | tf_op jit(solution)/shard_map/ppermute | solution.py:166
  45.6 29.4 %copy-start.1 = (f32[2,256,256]{2,1,0:T(8,128)S(1)}, f32[2,256,256]{2,1,0:T(8,128)}, u32[]{:S(2)}) copy-start(f32[2,256,256]{2,1,0:T(8,128)} %diag_inverse.1) | copy-start | bytes 1572868
  45.8 1.7 %collective-permute-start.2 = (f32[2,16,256]{2,1,0:T(8,128)S(1)}, f32[2,16,256]{2,1,0:T(8,128)S(1)}, u32[]{:S(2)}, u32[]{:S(2)}) collective-permute-start(f32[2,16,256]{2,1,0:T(8,128)S(1)} %get-tuple-element.14), channel_id=1, source_target_pairs={{0,8},{8,0},{16,24},{24,16},{32,40},{40,32},{48,56},{56,48},{64,72... | collective-permute-start | bytes 98312 | tf_op jit(solution)/shard_map/ppermute | solution.py:182
  70.9 4.1 %collective-permute-start.3 = (bf16[8,64,256]{2,1,0:T(8,128)(2,1)S(1)}, bf16[8,64,256]{2,1,0:T(8,128)(2,1)S(1)}, u32[]{:S(2)}, u32[]{:S(2)}) collective-permute-start(bf16[8,64,256]{2,1,0:T(8,128)(2,1)S(1)} %slice.4), channel_id=1, source_target_pairs={{0,8},{8,0},{16,24},{24,16},{32,40},{40,32},{48,56},{56,48},{64,72... | collective-permute-start | bytes 786440 | tf_op jit(solution)/shard_map/ppermute | solution.py:188

commit v2 on v1

--- a/solution.py
+++ b/solution.py
@@ -34,7 +34,10 @@
 SAME_CORE = [[row for row in range(16) if row % 2 == core] for core in range(2)]
 
 
-def pick_blocks(structure, panel, picks, chosen, sems):
+def pick_blocks(listed, panel, picks, chosen, structure, sems):
+    fetch = pltpu.make_async_copy(listed, structure, sems.at[0])
+    fetch.start()
+    fetch.wait()
     row, col = lax.axis_index("prow"), lax.axis_index("pcol")
     core = row & 1
     wanted = (row, col + 8 * core, col + 8 * (1 - core))
@@ -73,16 +76,31 @@
                 factor[s], blocks[s, i], (((0,), (1,)), ((), ())), preferred_element_type=jnp.float32
             )
             total = term if total is None else total + term
-        out[:, s] = (-total).reshape(8, 32, 512)
+        for d in range(8):
+            piece = -total[32 * d : 32 * d + 32]
+            largest = jnp.max(jnp.max(jnp.abs(piece), axis=0, keepdims=True), axis=1, keepdims=True)
+            exponent = jnp.ceil(jnp.log2(jnp.maximum(largest, 2.0**-120)))
+            scaled = jnp.clip(piece * jnp.exp2(-exponent) * 32767.0, -32767.0, 32767.0)
+            coded = jnp.round(scaled).astype(jnp.int32).astype(jnp.int16)
+            for k in range(4):
+                row = 64 * k + 32 * s
+                out[d, row : row + 32] = coded[:, 128 * k : 128 * k + 128]
+            tail = jnp.broadcast_to(exponent, (16, 128)).astype(jnp.int32).astype(jnp.int16)
+            out[d, 256 + 16 * s : 272 + 16 * s] = tail
 
 
 def round_and_project(arrived, chosen, columns, kept, sent):
     core = lax.axis_index("prow") & 1
     for s in range(2):
-        total = arrived[0, s]
-        for i in range(1, 8):
-            total += arrived[i, s]
-        rounded = total.astype(jnp.bfloat16)
+        total = [jnp.zeros((32, 128), jnp.float32)] * 4
+        for i in range(8):
+            tail = arrived[i, 256 + 16 * s : 272 + 16 * s].astype(jnp.int32).astype(jnp.float32)
+            scale = jnp.exp2(tail[:1]) * (1 / 32767.0)
+            for k in range(4):
+                row = 64 * k + 32 * s
+                coded = arrived[i, row : row + 32].astype(jnp.int32).astype(jnp.float32)
+                total[k] += coded * scale
+        rounded = jnp.concatenate(total, axis=1).astype(jnp.bfloat16)
         columns[s] = rounded
         term = jnp.dot(rounded, chosen[s], preferred_element_type=jnp.float32)
         first = core == 0
@@ -129,11 +147,11 @@
         off_diag[s, picks[s, 0]] = rows.astype(jnp.bfloat16)
 
 
-def call(body, out_shape, **rest):
+def call(body, out_shape, limit=VMEM_LIMIT, **rest):
     return pl.pallas_call(
         body,
         out_shape=out_shape,
-        compiler_params=pltpu.CompilerParams(vmem_limit_bytes=VMEM_LIMIT),
+        compiler_params=pltpu.CompilerParams(vmem_limit_bytes=limit),
         **rest,
     )
 
@@ -144,9 +162,10 @@
     picks, chosen = call(
         pick_blocks,
         (shape((2, 3), jnp.int32), shape((2, 512, 256), bf16)),
-        in_specs=[SMEM, HBM],
+        in_specs=[HBM, HBM],
         out_specs=(SMEM, ANY),
-        scratch_shapes=[pltpu.SemaphoreType.DMA((2,))],
+        scratch_shapes=[pltpu.SMEM((2, 16), jnp.int32), pltpu.SemaphoreType.DMA((2,))],
+        limit=62 * 1024 * 1024,
     )(structure, panel)
     own = lax.ppermute(chosen, BOTH, SPREAD)
     rows = 128
@@ -166,7 +185,7 @@
     other = lax.ppermute(own, "prow", SWAP)
     partial = call(
         multiply,
-        shape((8, 2, 32, 512), f32),
+        shape((8, 288, 128), jnp.int16),
         in_specs=[VMEM, VMEM, VMEM],
         out_specs=VMEM,
     )(blocks, own, other)

time: 77.1 us -> 87.4 us (1.13)
  Pallas kernels: 11.4 us -> 28.6 us
  blocking collectives: 48.7 us -> 43.6 us
  local copies, waits for them, and re-layouts: 2.28 us -> 0.71 us
    pallas_call x1, Pallas kernels: 1.34 us -> 18.3 us  [on_device(): call(pick_blocks, (shape((2, 3), jnp.int32), shape((2, 512, 256), bf16)),...]
    all_to_all x1, blocking collectives: 25.5 us -> 20.3 us  [on_device(): arrived = lax.all_to_all(partial, 'pcol', 0, 0)]
    unnamed x6 -> x8, local copies, waits for them, and re-layouts: 2.27 us -> 0.69 us
  transfers between devices with their start and end apart: 4 -> 4, of which waited for: 4 -> 4; matrix products, arithmetic and copies ran while one was open for 0% -> 0% of each run, Pallas kernels for 10% -> 9%
where the time goes in v2:
time: 87.4 us; the launch traced here: 87 us
  blocking collectives  43.6 us (50%)
  Pallas kernels  28.6 us (33%)
  starting transfers between devices  9.03 us (10%)
  waiting for transfers between devices  4.4 us (5%)
    all_to_all x1, blocking collectives, on_device(): arrived = lax.all_to_all(partial, 'pcol', 0, 0)  20.3 us
    pallas_call x1, Pallas kernels, on_device(): call(pick_blocks, (shape((2, 3), jnp.int32), shape((2, 512, 256), bf16)),...  18.3 us
    all_to_all x1, blocking collectives, on_device(): sums = lax.all_to_all(copies, 'prow', 0, 0, axis_index_groups=SAME_CORE)  13.8 us
    all_to_all x1, blocking collectives, on_device(): final = lax.all_to_all(packed, 'pcol', 0, 0)  9.53 us
    pallas_call x1, Pallas kernels, on_device(): call(extract, shape((2, 2, 512, 512), bf16), grid_spec=pltpu.PrefetchScal...  7.4 us
    ppermute x1, starting transfers between devices, on_device(): own = lax.ppermute(chosen, BOTH, SPREAD)  4.96 us
    ppermute x1, starting transfers between devices, on_device(): sibling = lax.ppermute(final[:, :64], 'prow', SWAP)  2.9 us
    ppermute x1, waiting for transfers between devices, on_device(): other = lax.ppermute(own, 'prow', SWAP)  1.91 us
  transfers between devices with their start and end apart: 4, of which 4 were waited for; matrix products, arithmetic and copies ran while one was open for 0% of the time, Pallas kernels for 9%

profile of v2, /device:TPU:1, one launch (start us, length us, event | category | flops | bytes accessed | tf_op | source)
XLA Modules:
  0.0 87.0 jit_solution(15012378070976517815)
XLA Ops:
  0.6 18.3 %shard_map.59 = (s32[2,3]{1,0:T(2,128)}, bf16[2,512,256]{2,1,0:T(8,128)(2,1)}) custom-call(s32[2,16]{1,0:T(2,128)} %listed.1, bf16[2,4,512,256]{3,2,1,0:T(8,128)(2,1)} %panel.1), custom_call_target="tpu_custom_call" | custom-call | tf_op jit(solution)/shard_map/pallas_call | solution.py:162
  18.9 5.0 %collective-permute-start = (bf16[2,512,256]{2,1,0:T(8,128)(2,1)}, bf16[2,512,256]{2,1,0:T(8,128)(2,1)S(1)}, u32[]{:S(2)}, u32[]{:S(2)}) collective-permute-start(bf16[2,512,256]{2,1,0:T(8,128)(2,1)} %get-tuple-element.10.chosen), channel_id=1, source_target_pairs={{0,64},{1,0},{2,32},{3,96},{4,80},{5,16},{6,48},{7,112},{8,97},{9,... | collective-permute-start | bytes 1572872 | tf_op jit(solution)/shard_map/ppermute | solution.py:170
  23.9 0.0 copy-start.2
  23.9 0.7 copy-done.2
  24.6 7.4 %shard_map.60.blocks = bf16[2,2,512,512]{3,2,1,0:T(8,128)(2,1)S(1)} custom-call(s32[2,3]{1,0:T(2,128)S(1)} %copy-done.2, bf16[4,512,8,512]{3,2,1,0:T(8,128)(2,1)} %block.1), custom_call_target="tpu_custom_call" | custom-call | bytes 10485760 | tf_op jit(solution)/shard_map/pallas_call | solution.py:172
  32.0 0.0 copy-start
  32.0 0.5 collective-permute-done.own
  32.5 0.0 collective-permute-start.1
  32.5 1.9 %collective-permute-done.1.other = bf16[2,512,256]{2,1,0:T(8,128)(2,1)S(1)} collective-permute-done((bf16[2,512,256]{2,1,0:T(8,128)(2,1)S(1)}, bf16[2,512,256]{2,1,0:T(8,128)(2,1)S(1)}, u32[]{:S(2)}, u32[]{:S(2)}) %collective-permute-start.1) | collective-permute-done | bytes 524320 | tf_op jit(solution)/shard_map/ppermute | solution.py:185
  34.4 0.9 %shard_map.61 = s16[8,288,128]{2,1,0:T(8,128)(2,1)S(1)} custom-call(bf16[2,2,512,512]{3,2,1,0:T(8,128)(2,1)S(1)} %shard_map.60.blocks, bf16[2,512,256]{2,1,0:T(8,128)(2,1)S(1)} %collective-permute-done.own, bf16[2,512,256]{2,1,0:T(8,128)(2,1)S(1)} %collective-permute-done.1.other), custom_call_target="tpu_custom_call" | custom-call | tf_op jit(solution)/shard_map/pallas_call | solution.py:186
  35.3 20.3 %all_to_all.15.arrived = s16[8,288,128]{2,1,0:T(8,128)(2,1)S(1)} all-to-all(s16[8,288,128]{2,1,0:T(8,128)(2,1)S(1)} %shard_map.61), channel_id=1, replica_groups=mesh['prow'=16,'pcol'=8] {'pcol'}, dimensions={0} | all-to-all | bytes 1179648 | tf_op jit(solution)/shard_map/all_to_all | solution.py:192
  55.6 0.0 copy-done
  55.6 0.0 copy-start.1
  55.6 0.0 copy-start.3
  55.6 0.3 shard_map.62
  55.8 1.2 %collective-permute-start.2 = (f32[2,16,256]{2,1,0:T(8,128)S(1)}, f32[2,16,256]{2,1,0:T(8,128)S(1)}, u32[]{:S(2)}, u32[]{:S(2)}) collective-permute-start(f32[2,16,256]{2,1,0:T(8,128)S(1)} %get-tuple-element.14), channel_id=1, source_target_pairs={{0,8},{8,0},{16,24},{24,16},{32,40},{40,32},{48,56},{56,48},{64,72... | collective-permute-start | bytes 98312 | tf_op jit(solution)/shard_map/ppermute | solution.py:201
  57.0 0.9 collective-permute-done.2.arrived
  57.9 13.8 %all_to_all.16.arrived = f32[8,2,16,256]{3,2,1,0:T(8,128)S(1)} all-to-all(f32[8,2,16,256]{3,2,1,0:T(8,128)S(1)} %shard_map.63), channel_id=1, replica_groups={{0,16,32,48,64,80,96,112},{8,24,40,56,72,88,104,120},{1,17,33,49,65,81,..., dimensions={0} | all-to-all | bytes 524288 | tf_op jit(solution)/shard_map/all_to_all | solution.py:202
  71.7 9.5 %all_to_all.17.own = bf16[8,96,256]{2,1,0:T(8,128)(2,1)S(1)} all-to-all(bf16[8,96,256]{2,1,0:T(8,128)(2,1)S(1)} %shard_map.64), channel_id=1, replica_groups=mesh['prow'=16,'pcol'=8] {'pcol'}, dimensions={0} | all-to-all | bytes 786432 | tf_op jit(solution)/shard_map/all_to_all | solution.py:206
  81.2 2.9 %collective-permute-start.3 = (bf16[8,64,256]{2,1,0:T(8,128)(2,1)S(1)}, bf16[8,64,256]{2,1,0:T(8,128)(2,1)S(1)}, u32[]{:S(2)}, u32[]{:S(2)}) collective-permute-start(bf16[8,64,256]{2,1,0:T(8,128)(2,1)S(1)} %slice.4), channel_id=1, source_target_pairs={{0,8},{8,0},{16,24},{24,16},{32,40},{40,32},{48,56},{56,48},{64,72... | collective-permute-start | bytes 786440 | tf_op jit(solution)/shard_map/ppermute | solution.py:207
  84.1 1.2 %collective-permute-done.3.other = bf16[8,64,256]{2,1,0:T(8,128)(2,1)S(1)} collective-permute-done((bf16[8,64,256]{2,1,0:T(8,128)(2,1)S(1)}, bf16[8,64,256]{2,1,0:T(8,128)(2,1)S(1)}, u32[]{:S(2)}, u32[]{:S(2)}) %collective-permute-start.3) | collective-permute-done | bytes 262176 | tf_op jit(solution)/shard_map/ppermute | solution.py:207
  85.3 0.0 copy-done.1
  85.3 0.0 copy-done.3
  85.3 1.7 %shard_map.65 = (bf16[2,4,64,256]{3,2,1,0:T(8,128)(2,1)}, f32[2,256,256]{2,1,0:T(8,128)}) custom-call(s32[2,3]{1,0:T(2,128)S(1)} %copy-done.3, bf16[8,96,256]{2,1,0:T(8,128)(2,1)S(1)} %all_to_all.17.own, bf16[8,64,256]{2,1,0:T(8,128)(2,1)S(1)} %collective-permute-done.3.other, f32[2,256,256]{2,1,0:T(8,128)S(1)} %copy-done.1), custom_call_target="tpu_custom_call" | custom-call | tf_op jit(solution)/shard_map/pallas_call | solution.py:208
  (3 shorter events, 0.1 us)
Async XLA Ops:
  18.9 13.5 %collective-permute-start = (bf16[2,512,256]{2,1,0:T(8,128)(2,1)}, bf16[2,512,256]{2,1,0:T(8,128)(2,1)S(1)}, u32[]{:S(2)}, u32[]{:S(2)}) collective-permute-start(bf16[2,512,256]{2,1,0:T(8,128)(2,1)} %get-tuple-element.10.chosen), channel_id=1, source_target_pairs={{0,64},{1,0},{2,32},{3,96},{4,80},{5,16},{6,48},{7,112},{8,97},{9,... | collective-permute-start | bytes 1572872 | tf_op jit(solution)/shard_map/ppermute | solution.py:170
  23.9 0.7 copy-start.2
  32.0 23.6 %copy-start = (bf16[2,512,256]{2,1,0:T(8,128)(2,1)S(1)}, bf16[2,512,256]{2,1,0:T(8,128)(2,1)}, u32[]{:S(2)}) copy-start(bf16[2,512,256]{2,1,0:T(8,128)(2,1)} %get-tuple-element.10.chosen) | copy-start | bytes 1572868
  32.5 1.9 %collective-permute-start.1 = (bf16[2,512,256]{2,1,0:T(8,128)(2,1)S(1)}, bf16[2,512,256]{2,1,0:T(8,128)(2,1)S(1)}, u32[]{:S(2)}, u32[]{:S(2)}) collective-permute-start(bf16[2,512,256]{2,1,0:T(8,128)(2,1)S(1)} %collective-permute-done.own), channel_id=1, source_target_pairs={{0,8},{8,0},{16,24},{24,16},{32,40},{40,32},{48,56},{56,48},{64,72... | collective-permute-start | bytes 1572872 | tf_op jit(solution)/shard_map/ppermute | solution.py:185
  55.6 29.7 %copy-start.1 = (f32[2,256,256]{2,1,0:T(8,128)S(1)}, f32[2,256,256]{2,1,0:T(8,128)}, u32[]{:S(2)}) copy-start(f32[2,256,256]{2,1,0:T(8,128)} %diag_inverse.1) | copy-start | bytes 1572868
  55.6 29.7 %copy-start.3 = (s32[2,3]{1,0:T(2,128)S(1)}, s32[2,3]{1,0:T(2,128)}, u32[]{:S(2)}) copy-start(s32[2,3]{1,0:T(2,128)} %get-tuple-element.9.picks) | copy-start | bytes 76
  55.8 2.0 %collective-permute-start.2 = (f32[2,16,256]{2,1,0:T(8,128)S(1)}, f32[2,16,256]{2,1,0:T(8,128)S(1)}, u32[]{:S(2)}, u32[]{:S(2)}) collective-permute-start(f32[2,16,256]{2,1,0:T(8,128)S(1)} %get-tuple-element.14), channel_id=1, source_target_pairs={{0,8},{8,0},{16,24},{24,16},{32,40},{40,32},{48,56},{56,48},{64,72... | collective-permute-start | bytes 98312 | tf_op jit(solution)/shard_map/ppermute | solution.py:201
  81.2 4.1 %collective-permute-start.3 = (bf16[8,64,256]{2,1,0:T(8,128)(2,1)S(1)}, bf16[8,64,256]{2,1,0:T(8,128)(2,1)S(1)}, u32[]{:S(2)}, u32[]{:S(2)}) collective-permute-start(bf16[8,64,256]{2,1,0:T(8,128)(2,1)S(1)} %slice.4), channel_id=1, source_target_pairs={{0,8},{8,0},{16,24},{24,16},{32,40},{40,32},{48,56},{56,48},{64,72... | collective-permute-start | bytes 786440 | tf_op jit(solution)/shard_map/ppermute | solution.py:207

commit v3 on v2

--- a/solution.py
+++ b/solution.py
@@ -163,9 +163,9 @@
         pick_blocks,
         (shape((2, 3), jnp.int32), shape((2, 512, 256), bf16)),
         in_specs=[HBM, HBM],
-        out_specs=(SMEM, ANY),
+        out_specs=(SMEM, VMEM),
         scratch_shapes=[pltpu.SMEM((2, 16), jnp.int32), pltpu.SemaphoreType.DMA((2,))],
-        limit=62 * 1024 * 1024,
+        limit=61 * 1024 * 1024,
     )(structure, panel)
     own = lax.ppermute(chosen, BOTH, SPREAD)
     rows = 128

time: 87.4 us -> 71.7 us (0.82)
  Pallas kernels: 28.6 us -> 12.9 us
    pallas_call x1, Pallas kernels: 18.3 us -> 2.61 us  [on_device(): call(pick_blocks, (shape((2, 3), jnp.int32), shape((2, 512, 256), bf16)),...]
  transfers between devices with their start and end apart: 4 -> 4, of which waited for: 4 -> 4; matrix products, arithmetic and copies ran while one was open for 0% -> 0% of each run, Pallas kernels for 9% -> 10%
where the time goes in v3:
time: 71.7 us; the launch traced here: 71.3 us
  blocking collectives  43.6 us (61%)
  Pallas kernels  12.9 us (18%)
  starting transfers between devices  9.03 us (13%)
  waiting for transfers between devices  4.42 us (6%)
    all_to_all x1, blocking collectives, on_device(): arrived = lax.all_to_all(partial, 'pcol', 0, 0)  20.3 us
    all_to_all x1, blocking collectives, on_device(): sums = lax.all_to_all(copies, 'prow', 0, 0, axis_index_groups=SAME_CORE)  13.8 us
    all_to_all x1, blocking collectives, on_device(): final = lax.all_to_all(packed, 'pcol', 0, 0)  9.53 us
    pallas_call x1, Pallas kernels, on_device(): call(extract, shape((2, 2, 512, 512), bf16), grid_spec=pltpu.PrefetchScal...  7.38 us
    ppermute x1, starting transfers between devices, on_device(): own = lax.ppermute(chosen, BOTH, SPREAD)  4.96 us
    ppermute x1, starting transfers between devices, on_device(): sibling = lax.ppermute(final[:, :64], 'prow', SWAP)  2.9 us
    pallas_call x1, Pallas kernels, on_device(): call(pick_blocks, (shape((2, 3), jnp.int32), shape((2, 512, 256), bf16)),...  2.61 us
    ppermute x1, waiting for transfers between devices, on_device(): other = lax.ppermute(own, 'prow', SWAP)  1.91 us
  transfers between devices with their start and end apart: 4, of which 4 were waited for; matrix products, arithmetic and copies ran while one was open for 0% of the time, Pallas kernels for 10%

profile of v3, /device:TPU:1, one launch (start us, length us, event | category | flops | bytes accessed | tf_op | source)
XLA Modules:
  0.0 71.3 jit_solution(8931341510883297801)
XLA Ops:
  0.6 2.6 %shard_map.59 = (s32[2,3]{1,0:T(2,128)}, bf16[2,512,256]{2,1,0:T(8,128)(2,1)}) custom-call(s32[2,16]{1,0:T(2,128)} %listed.1, bf16[2,4,512,256]{3,2,1,0:T(8,128)(2,1)} %panel.1), custom_call_target="tpu_custom_call" | custom-call | tf_op jit(solution)/shard_map/pallas_call | solution.py:162
  3.3 5.0 %collective-permute-start = (bf16[2,512,256]{2,1,0:T(8,128)(2,1)}, bf16[2,512,256]{2,1,0:T(8,128)(2,1)S(1)}, u32[]{:S(2)}, u32[]{:S(2)}) collective-permute-start(bf16[2,512,256]{2,1,0:T(8,128)(2,1)} %get-tuple-element.10.chosen), channel_id=1, source_target_pairs={{0,64},{1,0},{2,32},{3,96},{4,80},{5,16},{6,48},{7,112},{8,97},{9,... | collective-permute-start | bytes 1572872 | tf_op jit(solution)/shard_map/ppermute | solution.py:170
  8.2 0.0 copy-start.2
  8.2 0.7 copy-done.2
  8.9 7.4 %shard_map.60.blocks = bf16[2,2,512,512]{3,2,1,0:T(8,128)(2,1)S(1)} custom-call(s32[2,3]{1,0:T(2,128)S(1)} %copy-done.2, bf16[4,512,8,512]{3,2,1,0:T(8,128)(2,1)} %block.1), custom_call_target="tpu_custom_call" | custom-call | bytes 10485760 | tf_op jit(solution)/shard_map/pallas_call | solution.py:172
  16.3 0.0 copy-start
  16.3 0.5 collective-permute-done.own
  16.8 0.0 collective-permute-start.1
  16.8 1.9 %collective-permute-done.1.other = bf16[2,512,256]{2,1,0:T(8,128)(2,1)S(1)} collective-permute-done((bf16[2,512,256]{2,1,0:T(8,128)(2,1)S(1)}, bf16[2,512,256]{2,1,0:T(8,128)(2,1)S(1)}, u32[]{:S(2)}, u32[]{:S(2)}) %collective-permute-start.1) | collective-permute-done | bytes 524320 | tf_op jit(solution)/shard_map/ppermute | solution.py:185
  18.7 0.9 %shard_map.61 = s16[8,288,128]{2,1,0:T(8,128)(2,1)S(1)} custom-call(bf16[2,2,512,512]{3,2,1,0:T(8,128)(2,1)S(1)} %shard_map.60.blocks, bf16[2,512,256]{2,1,0:T(8,128)(2,1)S(1)} %collective-permute-done.own, bf16[2,512,256]{2,1,0:T(8,128)(2,1)S(1)} %collective-permute-done.1.other), custom_call_target="tpu_custom_call" | custom-call | tf_op jit(solution)/shard_map/pallas_call | solution.py:186
  19.6 20.3 %all_to_all.15.arrived = s16[8,288,128]{2,1,0:T(8,128)(2,1)S(1)} all-to-all(s16[8,288,128]{2,1,0:T(8,128)(2,1)S(1)} %shard_map.61), channel_id=1, replica_groups=mesh['prow'=16,'pcol'=8] {'pcol'}, dimensions={0} | all-to-all | bytes 1179648 | tf_op jit(solution)/shard_map/all_to_all | solution.py:192
  39.9 0.0 copy-done
  39.9 0.0 copy-start.1
  39.9 0.0 copy-start.3
  39.9 0.3 shard_map.62
  40.2 1.2 %collective-permute-start.2 = (f32[2,16,256]{2,1,0:T(8,128)S(1)}, f32[2,16,256]{2,1,0:T(8,128)S(1)}, u32[]{:S(2)}, u32[]{:S(2)}) collective-permute-start(f32[2,16,256]{2,1,0:T(8,128)S(1)} %get-tuple-element.14), channel_id=1, source_target_pairs={{0,8},{8,0},{16,24},{24,16},{32,40},{40,32},{48,56},{56,48},{64,72... | collective-permute-start | bytes 98312 | tf_op jit(solution)/shard_map/ppermute | solution.py:201
  41.3 0.9 %collective-permute-done.2.arrived = f32[2,16,256]{2,1,0:T(8,128)S(1)} collective-permute-done((f32[2,16,256]{2,1,0:T(8,128)S(1)}, f32[2,16,256]{2,1,0:T(8,128)S(1)}, u32[]{:S(2)}, u32[]{:S(2)}) %collective-permute-start.2) | collective-permute-done | bytes 32800 | tf_op jit(solution)/shard_map/ppermute | solution.py:201
  42.2 13.8 %all_to_all.16.arrived = f32[8,2,16,256]{3,2,1,0:T(8,128)S(1)} all-to-all(f32[8,2,16,256]{3,2,1,0:T(8,128)S(1)} %shard_map.63), channel_id=1, replica_groups={{0,16,32,48,64,80,96,112},{8,24,40,56,72,88,104,120},{1,17,33,49,65,81,..., dimensions={0} | all-to-all | bytes 524288 | tf_op jit(solution)/shard_map/all_to_all | solution.py:202
  56.0 9.5 %all_to_all.17.own = bf16[8,96,256]{2,1,0:T(8,128)(2,1)S(1)} all-to-all(bf16[8,96,256]{2,1,0:T(8,128)(2,1)S(1)} %shard_map.64), channel_id=1, replica_groups=mesh['prow'=16,'pcol'=8] {'pcol'}, dimensions={0} | all-to-all | bytes 786432 | tf_op jit(solution)/shard_map/all_to_all | solution.py:206
  65.6 2.9 %collective-permute-start.3 = (bf16[8,64,256]{2,1,0:T(8,128)(2,1)S(1)}, bf16[8,64,256]{2,1,0:T(8,128)(2,1)S(1)}, u32[]{:S(2)}, u32[]{:S(2)}) collective-permute-start(bf16[8,64,256]{2,1,0:T(8,128)(2,1)S(1)} %slice.4), channel_id=1, source_target_pairs={{0,8},{8,0},{16,24},{24,16},{32,40},{40,32},{48,56},{56,48},{64,72... | collective-permute-start | bytes 786440 | tf_op jit(solution)/shard_map/ppermute | solution.py:207
  68.5 1.2 %collective-permute-done.3.other = bf16[8,64,256]{2,1,0:T(8,128)(2,1)S(1)} collective-permute-done((bf16[8,64,256]{2,1,0:T(8,128)(2,1)S(1)}, bf16[8,64,256]{2,1,0:T(8,128)(2,1)S(1)}, u32[]{:S(2)}, u32[]{:S(2)}) %collective-permute-start.3) | collective-permute-done | bytes 262176 | tf_op jit(solution)/shard_map/ppermute | solution.py:207
  69.6 0.0 copy-done.1
  69.6 0.0 copy-done.3
  69.6 1.7 %shard_map.65 = (bf16[2,4,64,256]{3,2,1,0:T(8,128)(2,1)}, f32[2,256,256]{2,1,0:T(8,128)}) custom-call(s32[2,3]{1,0:T(2,128)S(1)} %copy-done.3, bf16[8,96,256]{2,1,0:T(8,128)(2,1)S(1)} %all_to_all.17.own, bf16[8,64,256]{2,1,0:T(8,128)(2,1)S(1)} %collective-permute-done.3.other, f32[2,256,256]{2,1,0:T(8,128)S(1)} %copy-done.1), custom_call_target="tpu_custom_call" | custom-call | tf_op jit(solution)/shard_map/pallas_call | solution.py:208
  (3 shorter events, 0.1 us)
Async XLA Ops:
  3.3 13.5 %collective-permute-start = (bf16[2,512,256]{2,1,0:T(8,128)(2,1)}, bf16[2,512,256]{2,1,0:T(8,128)(2,1)S(1)}, u32[]{:S(2)}, u32[]{:S(2)}) collective-permute-start(bf16[2,512,256]{2,1,0:T(8,128)(2,1)} %get-tuple-element.10.chosen), channel_id=1, source_target_pairs={{0,64},{1,0},{2,32},{3,96},{4,80},{5,16},{6,48},{7,112},{8,97},{9,... | collective-permute-start | bytes 1572872 | tf_op jit(solution)/shard_map/ppermute | solution.py:170
  8.2 0.7 copy-start.2
  16.3 23.6 %copy-start = (bf16[2,512,256]{2,1,0:T(8,128)(2,1)S(1)}, bf16[2,512,256]{2,1,0:T(8,128)(2,1)}, u32[]{:S(2)}) copy-start(bf16[2,512,256]{2,1,0:T(8,128)(2,1)} %get-tuple-element.10.chosen) | copy-start | bytes 1572868
  16.8 1.9 %collective-permute-start.1 = (bf16[2,512,256]{2,1,0:T(8,128)(2,1)S(1)}, bf16[2,512,256]{2,1,0:T(8,128)(2,1)S(1)}, u32[]{:S(2)}, u32[]{:S(2)}) collective-permute-start(bf16[2,512,256]{2,1,0:T(8,128)(2,1)S(1)} %collective-permute-done.own), channel_id=1, source_target_pairs={{0,8},{8,0},{16,24},{24,16},{32,40},{40,32},{48,56},{56,48},{64,72... | collective-permute-start | bytes 1572872 | tf_op jit(solution)/shard_map/ppermute | solution.py:185
  39.9 29.7 %copy-start.1 = (f32[2,256,256]{2,1,0:T(8,128)S(1)}, f32[2,256,256]{2,1,0:T(8,128)}, u32[]{:S(2)}) copy-start(f32[2,256,256]{2,1,0:T(8,128)} %diag_inverse.1) | copy-start | bytes 1572868
  39.9 29.7 %copy-start.3 = (s32[2,3]{1,0:T(2,128)S(1)}, s32[2,3]{1,0:T(2,128)}, u32[]{:S(2)}) copy-start(s32[2,3]{1,0:T(2,128)} %get-tuple-element.9.picks) | copy-start | bytes 76
  40.2 2.0 %collective-permute-start.2 = (f32[2,16,256]{2,1,0:T(8,128)S(1)}, f32[2,16,256]{2,1,0:T(8,128)S(1)}, u32[]{:S(2)}, u32[]{:S(2)}) collective-permute-start(f32[2,16,256]{2,1,0:T(8,128)S(1)} %get-tuple-element.14), channel_id=1, source_target_pairs={{0,8},{8,0},{16,24},{24,16},{32,40},{40,32},{48,56},{56,48},{64,72... | collective-permute-start | bytes 98312 | tf_op jit(solution)/shard_map/ppermute | solution.py:201
  65.6 4.1 %collective-permute-start.3 = (bf16[8,64,256]{2,1,0:T(8,128)(2,1)S(1)}, bf16[8,64,256]{2,1,0:T(8,128)(2,1)S(1)}, u32[]{:S(2)}, u32[]{:S(2)}) collective-permute-start(bf16[8,64,256]{2,1,0:T(8,128)(2,1)S(1)} %slice.4), channel_id=1, source_target_pairs={{0,8},{8,0},{16,24},{24,16},{32,40},{40,32},{48,56},{56,48},{64,72... | collective-permute-start | bytes 786440 | tf_op jit(solution)/shard_map/ppermute | solution.py:207

commit v4 on v3

--- a/solution.py
+++ b/solution.py
@@ -41,18 +41,19 @@
     row, col = lax.axis_index("prow"), lax.axis_index("pcol")
     core = row & 1
     wanted = (row, col + 8 * core, col + 8 * (1 - core))
+    lists = [[structure[s, k] for k in range(16)] for s in range(2)]
+
+    def place(s, i):
+        return sum(jnp.where((entry & 15) == wanted[i], entry >> 4, 0) for entry in lists[s])
+
     copies = []
     for s in range(2):
-        found = [jnp.int32(0)] * 3
-        for k in range(16):
-            entry = structure[s, k]
-            for i in range(3):
-                found[i] += jnp.where((entry & 15) == wanted[i], entry >> 4, 0)
-        copies.append(pltpu.make_async_copy(panel.at[s, found[0]], chosen.at[s], sems.at[s]))
+        picks[s, 0] = place(s, 0)
+        copies.append(pltpu.make_async_copy(panel.at[s, picks[s, 0]], chosen.at[s], sems.at[s]))
         copies[-1].start()
-        picks[s, 0] = found[0]
-        picks[s, 1] = 2 * found[1] + core
-        picks[s, 2] = 2 * found[2] + 1 - core
+    for s in range(2):
+        picks[s, 1] = 2 * place(s, 1) + core
+        picks[s, 2] = 2 * place(s, 2) + 1 - core
     for copy in copies:
         copy.wait()
 
@@ -127,10 +128,19 @@
             out[i, 64:, 128 * s : 128 * s + 128] = columns[s, :, i // 2 * 128 : i // 2 * 128 + 128]
 
 
-def finish(picks, own, other, diag_inverse, off_diag, diag_block):
-    core = lax.axis_index("prow") & 1
+def store_rows(picks, final, off_diag):
     half = lax.axis_index("pcol") & 1
     off_diag[...] = jnp.zeros_like(off_diag)
+    for s in range(2):
+        part = jnp.concatenate(
+            [final[i, 64:, 128 * s : 128 * s + 128].astype(jnp.float32) for i in range(8)], axis=0
+        ).T
+        rows = jnp.where(half == 0, part[:64], part[64:])
+        off_diag[s, picks[s, 0]] = rows.astype(jnp.bfloat16)
+
+
+def store_diag(own, other, diag_inverse, diag_block):
+    core = lax.axis_index("prow") & 1
     for s in range(2):
         slabs = []
         for i in range(8):
@@ -140,11 +150,6 @@
             slabs.append(jnp.where(core == 0, mine, theirs))
             slabs.append(jnp.where(core == 0, theirs, mine))
         diag_block[s] = diag_inverse[s] - jnp.concatenate(slabs, axis=0).T
-        part = jnp.concatenate(
-            [own[i, 64:, 128 * s : 128 * s + 128].astype(jnp.float32) for i in range(8)], axis=0
-        ).T
-        rows = jnp.where(half == 0, part[:64], part[64:])
-        off_diag[s, picks[s, 0]] = rows.astype(jnp.bfloat16)
 
 
 def call(body, out_shape, limit=VMEM_LIMIT, **rest):
@@ -159,13 +164,15 @@
 def on_device(inverse, panel, structure, diag_inverse):
     f32, bf16 = jnp.float32, jnp.bfloat16
     shape = jax.ShapeDtypeStruct
+    panel = pltpu.with_memory_space_constraint(panel, pltpu.HBM)
+    structure = pltpu.with_memory_space_constraint(structure, pltpu.HBM)
     picks, chosen = call(
         pick_blocks,
-        (shape((2, 3), jnp.int32), shape((2, 512, 256), bf16)),
+        (shape((2, 3), jnp.int32), pltpu.VMEM((2, 512, 256), bf16)),
         in_specs=[HBM, HBM],
         out_specs=(SMEM, VMEM),
         scratch_shapes=[pltpu.SMEM((2, 16), jnp.int32), pltpu.SemaphoreType.DMA((2,))],
-        limit=61 * 1024 * 1024,
+        limit=32 * 1024 * 1024,
     )(structure, panel)
     own = lax.ppermute(chosen, BOTH, SPREAD)
     rows = 128
@@ -205,12 +212,13 @@
     )(sums, columns)
     final = lax.all_to_all(packed, "pcol", 0, 0)
     sibling = lax.ppermute(final[:, :64], "prow", SWAP)
-    return call(
-        finish,
-        (shape((2, 4, 64, 256), bf16), shape((2, 256, 256), f32)),
-        in_specs=[SMEM, VMEM, VMEM, VMEM],
-        out_specs=(VMEM, VMEM),
-    )(picks, final, sibling, diag_inverse)
+    off_diag = call(
+        store_rows, shape((2, 4, 64, 256), bf16), in_specs=[SMEM, VMEM], out_specs=VMEM
+    )(picks, final)
+    diag_block = call(
+        store_diag, shape((2, 256, 256), f32), in_specs=[VMEM, VMEM, VMEM], out_specs=VMEM
+    )(final, sibling, diag_inverse)
+    return off_diag, diag_block
 
 
 def solution(mesh):

time: 71.7 us -> 70.8 us (0.987)
  waiting for transfers between devices: 4.42 us -> 3.6 us
    ppermute x1, waiting for transfers between devices: 1.16 us -> 0.01 us  [on_device(): sibling = lax.ppermute(final[:, :64], 'prow', SWAP)]
    pallas_call x2 -> x3, Pallas kernels: 4.3 us -> 4.77 us  [the longest x1 2.41 us: on_device(): call(pick_blocks, (shape((2, 3), jnp.int32), pltpu.VMEM((2, 512, 256), bf...]
  transfers between devices with their start and end apart: 4 -> 4, of which waited for: 4 -> 3; matrix products, arithmetic and copies ran while one was open for 0% -> 0% of each run, Pallas kernels for 10% -> 12%
where the time goes in v4:
time: 70.8 us; the launch traced here: 70.4 us
  blocking collectives  43.7 us (62%)
  Pallas kernels  13.4 us (19%)
  starting transfers between devices  9.03 us (13%)
  waiting for transfers between devices  3.6 us (5%)
    all_to_all x1, blocking collectives, on_device(): arrived = lax.all_to_all(partial, 'pcol', 0, 0)  20.4 us
    all_to_all x1, blocking collectives, on_device(): sums = lax.all_to_all(copies, 'prow', 0, 0, axis_index_groups=SAME_CORE)  13.8 us
    all_to_all x1, blocking collectives, on_device(): final = lax.all_to_all(packed, 'pcol', 0, 0)  9.53 us
    pallas_call x1, Pallas kernels, on_device(): call(extract, shape((2, 2, 512, 512), bf16), grid_spec=pltpu.PrefetchScal...  7.41 us
    ppermute x1, starting transfers between devices, on_device(): own = lax.ppermute(chosen, BOTH, SPREAD)  4.96 us
    ppermute x1, starting transfers between devices, on_device(): sibling = lax.ppermute(final[:, :64], 'prow', SWAP)  2.9 us
    pallas_call x1, Pallas kernels, on_device(): call(pick_blocks, (shape((2, 3), jnp.int32), pltpu.VMEM((2, 512, 256), bf...  2.41 us
    ppermute x1, waiting for transfers between devices, on_device(): other = lax.ppermute(own, 'prow', SWAP)  1.91 us
  transfers between devices with their start and end apart: 4, of which 3 were waited for; matrix products, arithmetic and copies ran while one was open for 0% of the time, Pallas kernels for 12%

profile of v4, /device:TPU:1, one launch (start us, length us, event | category | flops | bytes accessed | tf_op | source)
XLA Modules:
  0.0 70.4 jit_solution(963465880729939342)
XLA Ops:
  0.6 2.4 %shard_map.59 = (s32[2,3]{1,0:T(2,128)S(1)}, bf16[2,512,256]{2,1,0:T(8,128)(2,1)S(1)}) custom-call(s32[2,16]{1,0:T(2,128)} %listed.1, bf16[2,4,512,256]{3,2,1,0:T(8,128)(2,1)} %panel.1), custom_call_target="tpu_custom_call" | custom-call | tf_op jit(solution)/shard_map/pallas_call | solution.py:169
  3.0 5.0 %collective-permute-start = (bf16[2,512,256]{2,1,0:T(8,128)(2,1)S(1)}, bf16[2,512,256]{2,1,0:T(8,128)(2,1)S(1)}, u32[]{:S(2)}, u32[]{:S(2)}) collective-permute-start(bf16[2,512,256]{2,1,0:T(8,128)(2,1)S(1)} %get-tuple-element.10.chosen), channel_id=1, source_target_pairs={{0,64},{1,0},{2,32},{3,96},{4,80},{5,16},{6,48},{7,112},{8,97},{9,... | collective-permute-start | bytes 1572872 | tf_op jit(solution)/shard_map/ppermute | solution.py:177
  8.0 7.4 %shard_map.60.blocks = bf16[2,2,512,512]{3,2,1,0:T(8,128)(2,1)S(1)} custom-call(s32[2,3]{1,0:T(2,128)S(1)} %get-tuple-element.9.picks, bf16[4,512,8,512]{3,2,1,0:T(8,128)(2,1)} %block.1), custom_call_target="tpu_custom_call" | custom-call | bytes 10485760 | tf_op jit(solution)/shard_map/pallas_call | solution.py:179
  15.4 0.8 %collective-permute-done.own = bf16[2,512,256]{2,1,0:T(8,128)(2,1)S(1)} collective-permute-done((bf16[2,512,256]{2,1,0:T(8,128)(2,1)S(1)}, bf16[2,512,256]{2,1,0:T(8,128)(2,1)S(1)}, u32[]{:S(2)}, u32[]{:S(2)}) %collective-permute-start) | collective-permute-done | bytes 524320 | tf_op jit(solution)/shard_map/ppermute | solution.py:177
  16.3 0.0 collective-permute-start.1
  16.3 1.9 %collective-permute-done.1.other = bf16[2,512,256]{2,1,0:T(8,128)(2,1)S(1)} collective-permute-done((bf16[2,512,256]{2,1,0:T(8,128)(2,1)S(1)}, bf16[2,512,256]{2,1,0:T(8,128)(2,1)S(1)}, u32[]{:S(2)}, u32[]{:S(2)}) %collective-permute-start.1) | collective-permute-done | bytes 524320 | tf_op jit(solution)/shard_map/ppermute | solution.py:192
  18.2 0.9 %shard_map.61 = s16[8,288,128]{2,1,0:T(8,128)(2,1)S(1)} custom-call(bf16[2,2,512,512]{3,2,1,0:T(8,128)(2,1)S(1)} %shard_map.60.blocks, bf16[2,512,256]{2,1,0:T(8,128)(2,1)S(1)} %collective-permute-done.own, bf16[2,512,256]{2,1,0:T(8,128)(2,1)S(1)} %collective-permute-done.1.other), custom_call_target="tpu_custom_call" | custom-call | tf_op jit(solution)/shard_map/pallas_call | solution.py:193
  19.1 20.4 %all_to_all.15.arrived = s16[8,288,128]{2,1,0:T(8,128)(2,1)S(1)} all-to-all(s16[8,288,128]{2,1,0:T(8,128)(2,1)S(1)} %shard_map.61), channel_id=1, replica_groups=mesh['prow'=16,'pcol'=8] {'pcol'}, dimensions={0} | all-to-all | bytes 1179648 | tf_op jit(solution)/shard_map/all_to_all | solution.py:199
  39.5 0.0 copy-start
  39.5 0.3 shard_map.62
  39.7 1.2 %collective-permute-start.2 = (f32[2,16,256]{2,1,0:T(8,128)S(1)}, f32[2,16,256]{2,1,0:T(8,128)S(1)}, u32[]{:S(2)}, u32[]{:S(2)}) collective-permute-start(f32[2,16,256]{2,1,0:T(8,128)S(1)} %get-tuple-element.14), channel_id=1, source_target_pairs={{0,8},{8,0},{16,24},{24,16},{32,40},{40,32},{48,56},{56,48},{64,72... | collective-permute-start | bytes 98312 | tf_op jit(solution)/shard_map/ppermute | solution.py:208
  40.9 0.9 %collective-permute-done.2.arrived = f32[2,16,256]{2,1,0:T(8,128)S(1)} collective-permute-done((f32[2,16,256]{2,1,0:T(8,128)S(1)}, f32[2,16,256]{2,1,0:T(8,128)S(1)}, u32[]{:S(2)}, u32[]{:S(2)}) %collective-permute-start.2) | collective-permute-done | bytes 32800 | tf_op jit(solution)/shard_map/ppermute | solution.py:208
  41.8 13.8 %all_to_all.16.arrived = f32[8,2,16,256]{3,2,1,0:T(8,128)S(1)} all-to-all(f32[8,2,16,256]{3,2,1,0:T(8,128)S(1)} %shard_map.63), channel_id=1, replica_groups={{0,16,32,48,64,80,96,112},{8,24,40,56,72,88,104,120},{1,17,33,49,65,81,..., dimensions={0} | all-to-all | bytes 524288 | tf_op jit(solution)/shard_map/all_to_all | solution.py:209
  55.6 9.5 %all_to_all.17.final.own = bf16[8,96,256]{2,1,0:T(8,128)(2,1)S(1)} all-to-all(bf16[8,96,256]{2,1,0:T(8,128)(2,1)S(1)} %shard_map.64), channel_id=1, replica_groups=mesh['prow'=16,'pcol'=8] {'pcol'}, dimensions={0} | all-to-all | bytes 786432 | tf_op jit(solution)/shard_map/all_to_all | solution.py:213
  65.1 2.9 %collective-permute-start.3 = (bf16[8,64,256]{2,1,0:T(8,128)(2,1)S(1)}, bf16[8,64,256]{2,1,0:T(8,128)(2,1)S(1)}, u32[]{:S(2)}, u32[]{:S(2)}) collective-permute-start(bf16[8,64,256]{2,1,0:T(8,128)(2,1)S(1)} %slice.4), channel_id=1, source_target_pairs={{0,8},{8,0},{16,24},{24,16},{32,40},{40,32},{48,56},{56,48},{64,72... | collective-permute-start | bytes 786440 | tf_op jit(solution)/shard_map/ppermute | solution.py:214
  68.0 1.4 %shard_map.65 = bf16[2,4,64,256]{3,2,1,0:T(8,128)(2,1)} custom-call(s32[2,3]{1,0:T(2,128)S(1)} %get-tuple-element.9.picks, bf16[8,96,256]{2,1,0:T(8,128)(2,1)S(1)} %all_to_all.17.final.own), custom_call_target="tpu_custom_call" | custom-call | tf_op jit(solution)/shard_map/pallas_call | solution.py:215
  69.4 0.0 collective-permute-done.3.other
  69.4 0.0 copy-done
  69.4 1.0 %shard_map.66 = f32[2,256,256]{2,1,0:T(8,128)} custom-call(bf16[8,96,256]{2,1,0:T(8,128)(2,1)S(1)} %all_to_all.17.final.own, bf16[8,64,256]{2,1,0:T(8,128)(2,1)S(1)} %collective-permute-done.3.other, f32[2,256,256]{2,1,0:T(8,128)S(1)} %copy-done), custom_call_target="tpu_custom_call" | custom-call | tf_op jit(solution)/shard_map/pallas_call | solution.py:218
  (3 shorter events, 0.1 us)
Async XLA Ops:
  3.0 13.2 %collective-permute-start = (bf16[2,512,256]{2,1,0:T(8,128)(2,1)S(1)}, bf16[2,512,256]{2,1,0:T(8,128)(2,1)S(1)}, u32[]{:S(2)}, u32[]{:S(2)}) collective-permute-start(bf16[2,512,256]{2,1,0:T(8,128)(2,1)S(1)} %get-tuple-element.10.chosen), channel_id=1, source_target_pairs={{0,64},{1,0},{2,32},{3,96},{4,80},{5,16},{6,48},{7,112},{8,97},{9,... | collective-permute-start | bytes 1572872 | tf_op jit(solution)/shard_map/ppermute | solution.py:177
  16.3 1.9 %collective-permute-start.1 = (bf16[2,512,256]{2,1,0:T(8,128)(2,1)S(1)}, bf16[2,512,256]{2,1,0:T(8,128)(2,1)S(1)}, u32[]{:S(2)}, u32[]{:S(2)}) collective-permute-start(bf16[2,512,256]{2,1,0:T(8,128)(2,1)S(1)} %collective-permute-done.own), channel_id=1, source_target_pairs={{0,8},{8,0},{16,24},{24,16},{32,40},{40,32},{48,56},{56,48},{64,72... | collective-permute-start | bytes 1572872 | tf_op jit(solution)/shard_map/ppermute | solution.py:192
  39.5 29.9 %copy-start = (f32[2,256,256]{2,1,0:T(8,128)S(1)}, f32[2,256,256]{2,1,0:T(8,128)}, u32[]{:S(2)}) copy-start(f32[2,256,256]{2,1,0:T(8,128)} %diag_inverse.1) | copy-start | bytes 1572868
  39.7 2.0 %collective-permute-start.2 = (f32[2,16,256]{2,1,0:T(8,128)S(1)}, f32[2,16,256]{2,1,0:T(8,128)S(1)}, u32[]{:S(2)}, u32[]{:S(2)}) collective-permute-start(f32[2,16,256]{2,1,0:T(8,128)S(1)} %get-tuple-element.14), channel_id=1, source_target_pairs={{0,8},{8,0},{16,24},{24,16},{32,40},{40,32},{48,56},{56,48},{64,72... | collective-permute-start | bytes 98312 | tf_op jit(solution)/shard_map/ppermute | solution.py:208
  65.1 4.3 %collective-permute-start.3 = (bf16[8,64,256]{2,1,0:T(8,128)(2,1)S(1)}, bf16[8,64,256]{2,1,0:T(8,128)(2,1)S(1)}, u32[]{:S(2)}, u32[]{:S(2)}) collective-permute-start(bf16[8,64,256]{2,1,0:T(8,128)(2,1)S(1)} %slice.4), channel_id=1, source_target_pairs={{0,8},{8,0},{16,24},{24,16},{32,40},{40,32},{48,56},{56,48},{64,72... | collective-permute-start | bytes 786440 | tf_op jit(solution)/shard_map/ppermute | solution.py:214

commit v5 on v4

v5 whole, which is shorter than its diff:
```python
import functools

import jax
import jax.numpy as jnp
from jax import lax
from jax.experimental import pallas as pl
from jax.experimental.pallas import tpu as pltpu
from jax.sharding import PartitionSpec as P

BOTH = ("prow", "pcol")
SMEM = pl.BlockSpec(memory_space=pltpu.SMEM)
VMEM = pl.BlockSpec(memory_space=pltpu.VMEM)
ANY = pl.BlockSpec(memory_space=pl.ANY)
HBM = pl.BlockSpec(memory_space=pltpu.HBM)
VMEM_LIMIT = 48 * 1024 * 1024
SHIFT = (2, 0, 1, 3)


def spread():
    pairs = []
    for row in range(16):
        x, z_hi, core = row // 4, row // 2 % 2, row % 2
        for col in range(8):
            z_lo, y = col // 4, col % 4
            to_x = (x + SHIFT[(y - (z_hi * 2 + core)) % 4]) % 4
            to_z_hi = z_hi if z_lo == x % 2 else 1 - z_hi
            to_row = (to_x * 2 + to_z_hi) * 2 + x // 2
            pairs.append((row * 8 + col, to_row * 8 + row % 8))
    return pairs


SPREAD = spread()
SWAP = [(row, row ^ 1) for row in range(16)]
SAME_CORE = [[row for row in range(16) if row % 2 == core] for core in range(2)]


def pick_blocks(listed, panel, picks, chosen, structure, table, candidates, sems):
    fetch = pltpu.make_async_copy(listed, structure, sems.at[2])
    fetch.start()
    copies = [pltpu.make_async_copy(panel.at[s], candidates.at[s], sems.at[s]) for s in range(2)]
    for copy in copies:
        copy.start()
    fetch.wait()
    row, col = lax.axis_index("prow"), lax.axis_index("pcol")
    core = row & 1
    wanted = (row, col + 8 * core, col + 8 * (1 - core))
    for s in range(2):
        for k in range(16):
            entry = structure[s, k]
            table[s, entry & 15] = entry >> 4
    for s in range(2):
        picks[s, 0] = table[s, row]
        picks[s, 1] = 2 * table[s, wanted[1]] + core
        picks[s, 2] = 2 * table[s, wanted[2]] + 1 - core
    for s in range(2):
        copies[s].wait()
        chosen[s] = candidates[s, table[s, row]]


def extract(picks, block, out, wide):
    s = pl.program_id(0)
    rows = block.shape[1]
    for k in range(4):
        lanes = slice(128 * k, 128 * k + 128)
        wide[k] = block[0, :, :, lanes].astype(jnp.float32).reshape(rows * 8, 128)
        for i in range(2):
            column = wide[k, pl.ds(picks[s, 1 + i], rows, stride=8), :]
            out[0, i, :, lanes] = column.astype(jnp.bfloat16)


def to_code(piece):
    largest = jnp.max(jnp.max(jnp.abs(piece), axis=0, keepdims=True), axis=1, keepdims=True)
    exponent = jnp.ceil(jnp.log2(jnp.maximum(largest, 2.0**-120)))
    scaled = jnp.clip(piece * jnp.exp2(-exponent) * 32767.0, -32767.0, 32767.0)
    return jnp.round(scaled).astype(jnp.int32).astype(jnp.int16), exponent


def from_code(coded, tail):
    scale = jnp.exp2(tail.astype(jnp.int32).astype(jnp.float32)) * (1 / 32767.0)
    return coded.astype(jnp.int32).astype(jnp.float32) * scale


def tail_of(exponents, lanes):
    lane = lax.broadcasted_iota(jnp.int32, (8, lanes), 1) // (lanes // len(exponents))
    tail = jnp.zeros((8, lanes), jnp.float32)
    for i, exponent in enumerate(exponents):
        tail = jnp.where(lane == i, exponent, tail)
    return tail.astype(jnp.int32).astype(jnp.int16)


def multiply(blocks, own, other, out):
    exponents = [[] for _ in range(8)]
    for s in range(2):
        total = None
        for i, factor in enumerate((own, other)):
            term = lax.dot_general(
                factor[s], blocks[s, i], (((0,), (1,)), ((), ())), preferred_element_type=jnp.float32
            )
            total = term if total is None else total + term
        for d in range(8):
            coded, exponent = to_code(-total[32 * d : 32 * d + 32])
            exponents[d].append(exponent)
            for k in range(4):
                row = 64 * k + 32 * s
                out[d, row : row + 32] = coded[:, 128 * k : 128 * k + 128]
    for d in range(8):
        out[d, 256:] = tail_of(exponents[d], 128)


def round_and_project(arrived, chosen, columns, kept, sent):
    first = (lax.axis_index("prow") & 1) == 0
    for s in range(2):
        parts = []
        for k in range(4):
            row = 64 * k + 32 * s
            total = jnp.zeros((32, 128), jnp.float32)
            for i in range(8):
                total += from_code(arrived[i, row : row + 32], arrived[i, 256:257, 64 * s : 64 * s + 1])
            parts.append(total)
        total = jnp.concatenate(parts, axis=1)
        columns[s] = total
        term = jnp.dot(total.astype(jnp.bfloat16), chosen[s], preferred_element_type=jnp.float32)
        kept[s] = jnp.where(first, term[:16], term[16:])
        sent[s] = jnp.where(first, term[16:], term[:16])


def pair_sum(kept, arrived, out):
    coded, exponents = zip(*[to_code(kept[s] + arrived[s]) for s in range(2)])
    tail = tail_of(exponents, 128)
    for i in range(8):
        for s in range(2):
            out[i, 32 * s : 32 * s + 16] = coded[s][:, :128]
            out[i, 32 * s + 16 : 32 * s + 32] = coded[s][:, 128:]
        out[i, 64:] = tail


def pack(arrived, columns, out):
    exponents, whole = [], []
    for s in range(2):
        parts = []
        for k in range(2):
            row = 32 * s + 16 * k
            total = jnp.zeros((16, 128), jnp.float32)
            for i in range(8):
                total += from_code(arrived[i, row : row + 16], arrived[i, 64:65, 64 * s : 64 * s + 1])
            parts.append(total)
        coded, exponent = to_code(jnp.concatenate(parts, axis=1))
        exponents.append(exponent)
        for i in range(8):
            out[i, 16 * s : 16 * s + 16] = coded
    for s in range(2):
        coded, exponent = to_code(columns[s])
        exponents.append(exponent)
        whole.append(coded.astype(jnp.int32).astype(jnp.float32))
    tail = tail_of(exponents, 256)
    for i in range(8):
        piece = jnp.concatenate([part[:, 64 * i : 64 * i + 64] for part in whole], axis=1)
        piece = jnp.concatenate([piece[:16], piece[16:]], axis=1)
        out[i, 32:40] = tail
        out[i, 40:] = piece.astype(jnp.int32).astype(jnp.int16)


def store_rows(picks, final, off_diag):
    left = lax.broadcasted_iota(jnp.int32, (1, 128), 1) < 64
    slabs = []
    for i in range(8):
        tail = jnp.where(left, final[i, 32:33, 128:129].astype(jnp.int32), final[i, 32:33, 192:193].astype(jnp.int32))
        scale = jnp.exp2(tail.astype(jnp.float32)) * (1 / 32767.0)
        coded = final[i, 40:].astype(jnp.int32).astype(jnp.float32)
        slabs += [coded[:, :128] * scale, coded[:, 128:] * scale]
    rows = jnp.concatenate(slabs, axis=0).T
    for s in range(2):
        for r in range(4):
            off_diag[s, r] = jnp.where(picks[s : s + 1, :1] == r, rows[64 * s : 64 * s + 64], 0.0).astype(jnp.bfloat16)


def store_diag(own, other, diag_inverse, diag_block):
    first = (lax.axis_index("prow") & 1) == 0
    for s in range(2):
        rows, lane = slice(16 * s, 16 * s + 16), slice(64 * s, 64 * s + 1)
        slabs = []
        for i in range(8):
            mine = from_code(own[i, rows], own[i, 32:33, lane])
            theirs = from_code(other[i, rows], other[i, 32:33, lane])
            slabs += [jnp.where(first, mine, theirs), jnp.where(first, theirs, mine)]
        diag_block[s] = diag_inverse[s] - jnp.concatenate(slabs, axis=0).T


def call(body, out_shape, limit=VMEM_LIMIT, **rest):
    return pl.pallas_call(
        body,
        out_shape=out_shape,
        compiler_params=pltpu.CompilerParams(vmem_limit_bytes=limit),
        **rest,
    )


def on_device(inverse, panel, structure, diag_inverse):
    f32, bf16, i16 = jnp.float32, jnp.bfloat16, jnp.int16
    shape = jax.ShapeDtypeStruct
    panel = pltpu.with_memory_space_constraint(panel, pltpu.HBM)
    structure = pltpu.with_memory_space_constraint(structure, pltpu.HBM)
    picks, chosen = call(
        pick_blocks,
        (shape((2, 3), jnp.int32), pltpu.VMEM((2, 512, 256), bf16)),
        in_specs=[HBM, HBM],
        out_specs=(SMEM, VMEM),
        scratch_shapes=[
            pltpu.SMEM((2, 16), jnp.int32),
            pltpu.SMEM((2, 16), jnp.int32),
            pltpu.VMEM((2, 4, 512, 256), bf16),
            pltpu.SemaphoreType.DMA((3,)),
        ],
        limit=32 * 1024 * 1024,
    )(structure, panel)
    own = lax.ppermute(chosen, BOTH, SPREAD)
    rows = 128
    blocks = call(
        extract,
        shape((2, 2, 512, 512), bf16),
        grid_spec=pltpu.PrefetchScalarGridSpec(
            num_scalar_prefetch=1,
            grid=(2, 512 // rows),
            in_specs=[pl.BlockSpec((1, rows, 8, 512), lambda s, i, picks: (picks[s, 0], i, 0, 0))],
            out_specs=pl.BlockSpec((1, 2, rows, 512), lambda s, i, picks: (s, 0, i, 0)),
            scratch_shapes=[pltpu.VMEM((4, rows * 8, 128), f32)],
        ),
        cost_estimate=pl.CostEstimate(flops=0, bytes_accessed=10 << 20, transcendentals=0),
    )(picks, inverse)
    own, blocks = lax.optimization_barrier((own, blocks))
    other = lax.ppermute(own, "prow", SWAP)
    partial = call(
        multiply,
        shape((8, 264, 128), i16),
        in_specs=[VMEM, VMEM, VMEM],
        out_specs=VMEM,
    )(blocks, own, other)
    arrived = lax.all_to_all(partial, "pcol", 0, 0)
    columns, kept, sent = call(
        round_and_project,
        (shape((2, 32, 512), f32), shape((2, 16, 256), f32), shape((2, 16, 256), f32)),
        in_specs=[VMEM, VMEM],
        out_specs=(VMEM, VMEM, VMEM),
    )(arrived, chosen)
    copies = call(pair_sum, shape((8, 72, 128), i16), in_specs=[VMEM, VMEM], out_specs=VMEM)(
        kept, lax.ppermute(sent, "prow", SWAP)
    )
    sums = lax.all_to_all(copies, "prow", 0, 0, axis_index_groups=SAME_CORE)
    packed = call(pack, shape((8, 56, 256), i16), in_specs=[VMEM, VMEM], out_specs=VMEM)(sums, columns)
    final = lax.all_to_all(packed, "pcol", 0, 0)
    sibling = lax.ppermute(final[:, :40], "prow", SWAP)
    off_diag = call(
        store_rows, shape((2, 4, 64, 256), bf16), in_specs=[VMEM, VMEM], out_specs=VMEM
    )(picks, final)
    diag_block = call(
        store_diag, shape((2, 256, 256), f32), in_specs=[VMEM, VMEM, VMEM], out_specs=VMEM
    )(final, sibling, diag_inverse)
    return off_diag, diag_block


def solution(mesh):
    placed = (P(None, "prow", None, "pcol"), P(None, None, "prow", None), P(), P())
    return jax.shard_map(
        on_device,
        mesh=mesh,
        in_specs=placed,
        out_specs=(P(None, None, ("prow", "pcol"), None), P()),
        check_vma=False,
    )
```

time: 70.8 us -> 68.7 us (0.970)
  blocking collectives: 43.7 us -> 41.9 us
    all_to_all x1, blocking collectives: 9.53 us -> 8.47 us  [on_device(): final = lax.all_to_all(packed, 'pcol', 0, 0)]
  transfers between devices with their start and end apart: 4 -> 4, of which waited for: 3 -> 4; matrix products, arithmetic and copies ran while one was open for 0% -> 0% of each run, Pallas kernels for 12% -> 12%
where the time goes in v5:
time: 68.7 us; the launch traced here: 68.3 us
  blocking collectives  41.9 us (61%)
  Pallas kernels  13.2 us (19%)
  starting transfers between devices  8.83 us (13%)
  waiting for transfers between devices  3.74 us (5%)
    all_to_all x1, blocking collectives, on_device(): arrived = lax.all_to_all(partial, 'pcol', 0, 0)  20.1 us
    all_to_all x1, blocking collectives, on_device(): sums = lax.all_to_all(copies, 'prow', 0, 0, axis_index_groups=SAME_CORE)  13.3 us
    all_to_all x1, blocking collectives, on_device(): final = lax.all_to_all(packed, 'pcol', 0, 0)  8.47 us
    pallas_call x1, Pallas kernels, on_device(): call(extract, shape((2, 2, 512, 512), bf16), grid_spec=pltpu.PrefetchScal...  7.41 us
    ppermute x1, starting transfers between devices, on_device(): own = lax.ppermute(chosen, BOTH, SPREAD)  4.96 us
    ppermute x1, starting transfers between devices, on_device(): sibling = lax.ppermute(final[:, :40], 'prow', SWAP)  2.71 us
    pallas_call x1, Pallas kernels, on_device(): call(pick_blocks, (shape((2, 3), jnp.int32), pltpu.VMEM((2, 512, 256), bf...  2.17 us
    ppermute x1, waiting for transfers between devices, on_device(): other = lax.ppermute(own, 'prow', SWAP)  1.91 us
  transfers between devices with their start and end apart: 4, of which 4 were waited for; matrix products, arithmetic and copies ran while one was open for 0% of the time, Pallas kernels for 12%

profile of v5, /device:TPU:1, one launch (start us, length us, event | category | flops | bytes accessed | tf_op | source)
XLA Modules:
  0.0 68.3 jit_solution(9050605797384335615)
XLA Ops:
  0.6 2.2 %shard_map.59 = (s32[2,3]{1,0:T(2,128)S(1)}, bf16[2,512,256]{2,1,0:T(8,128)(2,1)S(1)}) custom-call(s32[2,16]{1,0:T(2,128)} %listed.1, bf16[2,4,512,256]{3,2,1,0:T(8,128)(2,1)} %panel.1), custom_call_target="tpu_custom_call" | custom-call | tf_op jit(solution)/shard_map/pallas_call | solution.py:203
  2.8 5.0 %collective-permute-start = (bf16[2,512,256]{2,1,0:T(8,128)(2,1)S(1)}, bf16[2,512,256]{2,1,0:T(8,128)(2,1)S(1)}, u32[]{:S(2)}, u32[]{:S(2)}) collective-permute-start(bf16[2,512,256]{2,1,0:T(8,128)(2,1)S(1)} %get-tuple-element.10.chosen), channel_id=1, source_target_pairs={{0,64},{1,0},{2,32},{3,96},{4,80},{5,16},{6,48},{7,112},{8,97},{9,... | collective-permute-start | bytes 1572872 | tf_op jit(solution)/shard_map/ppermute | solution.py:216
  7.8 7.4 %shard_map.60.blocks = bf16[2,2,512,512]{3,2,1,0:T(8,128)(2,1)S(1)} custom-call(s32[2,3]{1,0:T(2,128)S(1)} %get-tuple-element.9.picks, bf16[4,512,8,512]{3,2,1,0:T(8,128)(2,1)} %block.1), custom_call_target="tpu_custom_call" | custom-call | bytes 10485760 | tf_op jit(solution)/shard_map/pallas_call | solution.py:218
  15.2 0.8 %collective-permute-done.own = bf16[2,512,256]{2,1,0:T(8,128)(2,1)S(1)} collective-permute-done((bf16[2,512,256]{2,1,0:T(8,128)(2,1)S(1)}, bf16[2,512,256]{2,1,0:T(8,128)(2,1)S(1)}, u32[]{:S(2)}, u32[]{:S(2)}) %collective-permute-start) | collective-permute-done | bytes 524320 | tf_op jit(solution)/shard_map/ppermute | solution.py:216
  16.0 0.0 collective-permute-start.1
  16.0 1.9 %collective-permute-done.1.other = bf16[2,512,256]{2,1,0:T(8,128)(2,1)S(1)} collective-permute-done((bf16[2,512,256]{2,1,0:T(8,128)(2,1)S(1)}, bf16[2,512,256]{2,1,0:T(8,128)(2,1)S(1)}, u32[]{:S(2)}, u32[]{:S(2)}) %collective-permute-start.1) | collective-permute-done | bytes 524320 | tf_op jit(solution)/shard_map/ppermute | solution.py:231
  17.9 0.9 %shard_map.61 = s16[8,264,128]{2,1,0:T(8,128)(2,1)S(1)} custom-call(bf16[2,2,512,512]{3,2,1,0:T(8,128)(2,1)S(1)} %shard_map.60.blocks, bf16[2,512,256]{2,1,0:T(8,128)(2,1)S(1)} %collective-permute-done.own, bf16[2,512,256]{2,1,0:T(8,128)(2,1)S(1)} %collective-permute-done.1.other), custom_call_target="tpu_custom_call" | custom-call | tf_op jit(solution)/shard_map/pallas_call | solution.py:232
  18.8 0.0 copy-start
  18.9 20.1 %all_to_all.15.arrived = s16[8,264,128]{2,1,0:T(8,128)(2,1)S(1)} all-to-all(s16[8,264,128]{2,1,0:T(8,128)(2,1)S(1)} %shard_map.61), channel_id=1, replica_groups=mesh['prow'=16,'pcol'=8] {'pcol'}, dimensions={0} | all-to-all | bytes 1081344 | tf_op jit(solution)/shard_map/all_to_all | solution.py:238
  38.9 0.3 shard_map.62
  39.2 1.2 %collective-permute-start.2 = (f32[2,16,256]{2,1,0:T(8,128)S(1)}, f32[2,16,256]{2,1,0:T(8,128)S(1)}, u32[]{:S(2)}, u32[]{:S(2)}) collective-permute-start(f32[2,16,256]{2,1,0:T(8,128)S(1)} %get-tuple-element.14), channel_id=1, source_target_pairs={{0,8},{8,0},{16,24},{24,16},{32,40},{40,32},{48,56},{56,48},{64,72... | collective-permute-start | bytes 98312 | tf_op jit(solution)/shard_map/ppermute | solution.py:246
  40.4 0.9 %collective-permute-done.2.arrived = f32[2,16,256]{2,1,0:T(8,128)S(1)} collective-permute-done((f32[2,16,256]{2,1,0:T(8,128)S(1)}, f32[2,16,256]{2,1,0:T(8,128)S(1)}, u32[]{:S(2)}, u32[]{:S(2)}) %collective-permute-start.2) | collective-permute-done | bytes 32800 | tf_op jit(solution)/shard_map/ppermute | solution.py:246
  41.2 0.1 shard_map.63
  41.4 13.3 %all_to_all.16.arrived = s16[8,72,128]{2,1,0:T(8,128)(2,1)S(1)} all-to-all(s16[8,72,128]{2,1,0:T(8,128)(2,1)S(1)} %shard_map.63), channel_id=1, replica_groups={{0,16,32,48,64,80,96,112},{8,24,40,56,72,88,104,120},{1,17,33,49,65,81,..., dimensions={0} | all-to-all | bytes 294912 | tf_op jit(solution)/shard_map/all_to_all | solution.py:248
  54.7 0.3 shard_map.64
  55.0 8.5 %all_to_all.17.final.own = s16[8,56,256]{2,1,0:T(8,128)(2,1)S(1)} all-to-all(s16[8,56,256]{2,1,0:T(8,128)(2,1)S(1)} %shard_map.64), channel_id=1, replica_groups=mesh['prow'=16,'pcol'=8] {'pcol'}, dimensions={0} | all-to-all | bytes 458752 | tf_op jit(solution)/shard_map/all_to_all | solution.py:250
  63.5 2.7 %collective-permute-start.3 = (s16[8,40,256]{2,1,0:T(8,128)(2,1)S(1)}, s16[8,40,256]{2,1,0:T(8,128)(2,1)S(1)}, u32[]{:S(2)}, u32[]{:S(2)}) collective-permute-start(s16[8,40,256]{2,1,0:T(8,128)(2,1)S(1)} %slice.4), channel_id=1, source_target_pairs={{0,8},{8,0},{16,24},{24,16},{32,40},{40,32},{48,56},{56,48},{64,72... | collective-permute-start | bytes 491528 | tf_op jit(solution)/shard_map/ppermute | solution.py:251
  66.2 0.9 %shard_map.65 = bf16[2,4,64,256]{3,2,1,0:T(8,128)(2,1)} custom-call(s32[2,3]{1,0:T(2,128)S(1)} %get-tuple-element.9.picks, s16[8,56,256]{2,1,0:T(8,128)(2,1)S(1)} %all_to_all.17.final.own), custom_call_target="tpu_custom_call" | custom-call | tf_op jit(solution)/shard_map/pallas_call | solution.py:252
  67.1 0.1 collective-permute-done.3.other
  67.3 0.0 copy-done
  67.3 1.1 %shard_map.66 = f32[2,256,256]{2,1,0:T(8,128)} custom-call(s16[8,56,256]{2,1,0:T(8,128)(2,1)S(1)} %all_to_all.17.final.own, s16[8,40,256]{2,1,0:T(8,128)(2,1)S(1)} %collective-permute-done.3.other, f32[2,256,256]{2,1,0:T(8,128)S(1)} %copy-done), custom_call_target="tpu_custom_call" | custom-call | tf_op jit(solution)/shard_map/pallas_call | solution.py:255
  (1 shorter events, 0.0 us)
Async XLA Ops:
  2.8 13.2 %collective-permute-start = (bf16[2,512,256]{2,1,0:T(8,128)(2,1)S(1)}, bf16[2,512,256]{2,1,0:T(8,128)(2,1)S(1)}, u32[]{:S(2)}, u32[]{:S(2)}) collective-permute-start(bf16[2,512,256]{2,1,0:T(8,128)(2,1)S(1)} %get-tuple-element.10.chosen), channel_id=1, source_target_pairs={{0,64},{1,0},{2,32},{3,96},{4,80},{5,16},{6,48},{7,112},{8,97},{9,... | collective-permute-start | bytes 1572872 | tf_op jit(solution)/shard_map/ppermute | solution.py:216
  16.0 1.9 %collective-permute-start.1 = (bf16[2,512,256]{2,1,0:T(8,128)(2,1)S(1)}, bf16[2,512,256]{2,1,0:T(8,128)(2,1)S(1)}, u32[]{:S(2)}, u32[]{:S(2)}) collective-permute-start(bf16[2,512,256]{2,1,0:T(8,128)(2,1)S(1)} %collective-permute-done.own), channel_id=1, source_target_pairs={{0,8},{8,0},{16,24},{24,16},{32,40},{40,32},{48,56},{56,48},{64,72... | collective-permute-start | bytes 1572872 | tf_op jit(solution)/shard_map/ppermute | solution.py:231
  18.8 48.4 %copy-start = (f32[2,256,256]{2,1,0:T(8,128)S(1)}, f32[2,256,256]{2,1,0:T(8,128)}, u32[]{:S(2)}) copy-start(f32[2,256,256]{2,1,0:T(8,128)} %diag_inverse.1) | copy-start | bytes 1572868
  39.2 2.0 %collective-permute-start.2 = (f32[2,16,256]{2,1,0:T(8,128)S(1)}, f32[2,16,256]{2,1,0:T(8,128)S(1)}, u32[]{:S(2)}, u32[]{:S(2)}) collective-permute-start(f32[2,16,256]{2,1,0:T(8,128)S(1)} %get-tuple-element.14), channel_id=1, source_target_pairs={{0,8},{8,0},{16,24},{24,16},{32,40},{40,32},{48,56},{56,48},{64,72... | collective-permute-start | bytes 98312 | tf_op jit(solution)/shard_map/ppermute | solution.py:246
  63.5 3.7 %collective-permute-start.3 = (s16[8,40,256]{2,1,0:T(8,128)(2,1)S(1)}, s16[8,40,256]{2,1,0:T(8,128)(2,1)S(1)}, u32[]{:S(2)}, u32[]{:S(2)}) collective-permute-start(s16[8,40,256]{2,1,0:T(8,128)(2,1)S(1)} %slice.4), channel_id=1, source_target_pairs={{0,8},{8,0},{16,24},{24,16},{32,40},{40,32},{48,56},{56,48},{64,72... | collective-permute-start | bytes 491528 | tf_op jit(solution)/shard_map/ppermute | solution.py:251

commit v6 on v5

--- a/solution.py
+++ b/solution.py
@@ -174,8 +174,9 @@
             off_diag[s, r] = jnp.where(picks[s : s + 1, :1] == r, rows[64 * s : 64 * s + 64], 0.0).astype(jnp.bfloat16)
 
 
-def store_diag(own, other, diag_inverse, diag_block):
+def store_diag(own, other, diag_inverse, diag_block, result, sems):
     first = (lax.axis_index("prow") & 1) == 0
+    copies = []
     for s in range(2):
         rows, lane = slice(16 * s, 16 * s + 16), slice(64 * s, 64 * s + 1)
         slabs = []
@@ -183,7 +184,11 @@
             mine = from_code(own[i, rows], own[i, 32:33, lane])
             theirs = from_code(other[i, rows], other[i, 32:33, lane])
             slabs += [jnp.where(first, mine, theirs), jnp.where(first, theirs, mine)]
-        diag_block[s] = diag_inverse[s] - jnp.concatenate(slabs, axis=0).T
+        result[s] = diag_inverse[s] - jnp.concatenate(slabs, axis=0).T
+        copies.append(pltpu.make_async_copy(result.at[s], diag_block.at[s], sems.at[s]))
+        copies[-1].start()
+    for copy in copies:
+        copy.wait()
 
 
 def call(body, out_shape, limit=VMEM_LIMIT, **rest):
@@ -253,7 +258,11 @@
         store_rows, shape((2, 4, 64, 256), bf16), in_specs=[VMEM, VMEM], out_specs=VMEM
     )(picks, final)
     diag_block = call(
-        store_diag, shape((2, 256, 256), f32), in_specs=[VMEM, VMEM, VMEM], out_specs=VMEM
+        store_diag,
+        shape((2, 256, 256), f32),
+        in_specs=[VMEM, VMEM, VMEM],
+        out_specs=HBM,
+        scratch_shapes=[pltpu.VMEM((2, 256, 256), f32), pltpu.SemaphoreType.DMA((2,))],
     )(final, sibling, diag_inverse)
     return off_diag, diag_block
 

time: 68.7 us -> 68.6 us (level)
  no operation moved by 1% of the time
where the time goes in v6:
time: 68.6 us; the launch traced here: 68.3 us
  blocking collectives  41.9 us (61%)
  Pallas kernels  13.1 us (19%)
  starting transfers between devices  8.83 us (13%)
  waiting for transfers between devices  3.76 us (5%)
    all_to_all x1, blocking collectives, on_device(): arrived = lax.all_to_all(partial, 'pcol', 0, 0)  20.1 us
    all_to_all x1, blocking collectives, on_device(): sums = lax.all_to_all(copies, 'prow', 0, 0, axis_index_groups=SAME_CORE)  13.3 us
    all_to_all x1, blocking collectives, on_device(): final = lax.all_to_all(packed, 'pcol', 0, 0)  8.47 us
    pallas_call x1, Pallas kernels, on_device(): call(extract, shape((2, 2, 512, 512), bf16), grid_spec=pltpu.PrefetchScal...  7.39 us
    ppermute x1, starting transfers between devices, on_device(): own = lax.ppermute(chosen, BOTH, SPREAD)  4.96 us
    ppermute x1, starting transfers between devices, on_device(): sibling = lax.ppermute(final[:, :40], 'prow', SWAP)  2.71 us
    pallas_call x1, Pallas kernels, on_device(): call(pick_blocks, (shape((2, 3), jnp.int32), pltpu.VMEM((2, 512, 256), bf...  2.17 us
    ppermute x1, waiting for transfers between devices, on_device(): other = lax.ppermute(own, 'prow', SWAP)  1.91 us
  transfers between devices with their start and end apart: 4, of which 4 were waited for; matrix products, arithmetic and copies ran while one was open for 0% of the time, Pallas kernels for 12%

profile of v6, /device:TPU:1, one launch (start us, length us, event | category | flops | bytes accessed | tf_op | source)
XLA Modules:
  0.0 68.3 jit_solution(484566474811663556)
XLA Ops:
  0.6 2.2 %shard_map.59 = (s32[2,3]{1,0:T(2,128)S(1)}, bf16[2,512,256]{2,1,0:T(8,128)(2,1)S(1)}) custom-call(s32[2,16]{1,0:T(2,128)} %listed.1, bf16[2,4,512,256]{3,2,1,0:T(8,128)(2,1)} %panel.1), custom_call_target="tpu_custom_call" | custom-call | tf_op jit(solution)/shard_map/pallas_call | solution.py:208
  2.8 5.0 %collective-permute-start = (bf16[2,512,256]{2,1,0:T(8,128)(2,1)S(1)}, bf16[2,512,256]{2,1,0:T(8,128)(2,1)S(1)}, u32[]{:S(2)}, u32[]{:S(2)}) collective-permute-start(bf16[2,512,256]{2,1,0:T(8,128)(2,1)S(1)} %get-tuple-element.10.chosen), channel_id=1, source_target_pairs={{0,64},{1,0},{2,32},{3,96},{4,80},{5,16},{6,48},{7,112},{8,97},{9,... | collective-permute-start | bytes 1572872 | tf_op jit(solution)/shard_map/ppermute | solution.py:221
  7.8 7.4 %shard_map.60.blocks = bf16[2,2,512,512]{3,2,1,0:T(8,128)(2,1)S(1)} custom-call(s32[2,3]{1,0:T(2,128)S(1)} %get-tuple-element.9.picks, bf16[4,512,8,512]{3,2,1,0:T(8,128)(2,1)} %block.1), custom_call_target="tpu_custom_call" | custom-call | bytes 10485760 | tf_op jit(solution)/shard_map/pallas_call | solution.py:223
  15.2 0.9 %collective-permute-done.own = bf16[2,512,256]{2,1,0:T(8,128)(2,1)S(1)} collective-permute-done((bf16[2,512,256]{2,1,0:T(8,128)(2,1)S(1)}, bf16[2,512,256]{2,1,0:T(8,128)(2,1)S(1)}, u32[]{:S(2)}, u32[]{:S(2)}) %collective-permute-start) | collective-permute-done | bytes 524320 | tf_op jit(solution)/shard_map/ppermute | solution.py:221
  16.0 0.0 collective-permute-start.1
  16.0 1.9 %collective-permute-done.1.other = bf16[2,512,256]{2,1,0:T(8,128)(2,1)S(1)} collective-permute-done((bf16[2,512,256]{2,1,0:T(8,128)(2,1)S(1)}, bf16[2,512,256]{2,1,0:T(8,128)(2,1)S(1)}, u32[]{:S(2)}, u32[]{:S(2)}) %collective-permute-start.1) | collective-permute-done | bytes 524320 | tf_op jit(solution)/shard_map/ppermute | solution.py:236
  17.9 0.9 %shard_map.61 = s16[8,264,128]{2,1,0:T(8,128)(2,1)S(1)} custom-call(bf16[2,2,512,512]{3,2,1,0:T(8,128)(2,1)S(1)} %shard_map.60.blocks, bf16[2,512,256]{2,1,0:T(8,128)(2,1)S(1)} %collective-permute-done.own, bf16[2,512,256]{2,1,0:T(8,128)(2,1)S(1)} %collective-permute-done.1.other), custom_call_target="tpu_custom_call" | custom-call | tf_op jit(solution)/shard_map/pallas_call | solution.py:237
  18.8 0.0 copy-start
  18.9 20.1 %all_to_all.15.arrived = s16[8,264,128]{2,1,0:T(8,128)(2,1)S(1)} all-to-all(s16[8,264,128]{2,1,0:T(8,128)(2,1)S(1)} %shard_map.61), channel_id=1, replica_groups=mesh['prow'=16,'pcol'=8] {'pcol'}, dimensions={0} | all-to-all | bytes 1081344 | tf_op jit(solution)/shard_map/all_to_all | solution.py:243
  38.9 0.3 shard_map.62
  39.2 1.2 %collective-permute-start.2 = (f32[2,16,256]{2,1,0:T(8,128)S(1)}, f32[2,16,256]{2,1,0:T(8,128)S(1)}, u32[]{:S(2)}, u32[]{:S(2)}) collective-permute-start(f32[2,16,256]{2,1,0:T(8,128)S(1)} %get-tuple-element.14), channel_id=1, source_target_pairs={{0,8},{8,0},{16,24},{24,16},{32,40},{40,32},{48,56},{56,48},{64,72... | collective-permute-start | bytes 98312 | tf_op jit(solution)/shard_map/ppermute | solution.py:251
  40.4 0.9 %collective-permute-done.2.arrived = f32[2,16,256]{2,1,0:T(8,128)S(1)} collective-permute-done((f32[2,16,256]{2,1,0:T(8,128)S(1)}, f32[2,16,256]{2,1,0:T(8,128)S(1)}, u32[]{:S(2)}, u32[]{:S(2)}) %collective-permute-start.2) | collective-permute-done | bytes 32800 | tf_op jit(solution)/shard_map/ppermute | solution.py:251
  41.2 0.1 shard_map.63
  41.4 13.3 %all_to_all.16.arrived = s16[8,72,128]{2,1,0:T(8,128)(2,1)S(1)} all-to-all(s16[8,72,128]{2,1,0:T(8,128)(2,1)S(1)} %shard_map.63), channel_id=1, replica_groups={{0,16,32,48,64,80,96,112},{8,24,40,56,72,88,104,120},{1,17,33,49,65,81,..., dimensions={0} | all-to-all | bytes 294912 | tf_op jit(solution)/shard_map/all_to_all | solution.py:253
  54.7 0.3 shard_map.64
  55.0 8.5 %all_to_all.17.final.own = s16[8,56,256]{2,1,0:T(8,128)(2,1)S(1)} all-to-all(s16[8,56,256]{2,1,0:T(8,128)(2,1)S(1)} %shard_map.64), channel_id=1, replica_groups=mesh['prow'=16,'pcol'=8] {'pcol'}, dimensions={0} | all-to-all | bytes 458752 | tf_op jit(solution)/shard_map/all_to_all | solution.py:255
  63.5 2.7 %collective-permute-start.3 = (s16[8,40,256]{2,1,0:T(8,128)(2,1)S(1)}, s16[8,40,256]{2,1,0:T(8,128)(2,1)S(1)}, u32[]{:S(2)}, u32[]{:S(2)}) collective-permute-start(s16[8,40,256]{2,1,0:T(8,128)(2,1)S(1)} %slice.4), channel_id=1, source_target_pairs={{0,8},{8,0},{16,24},{24,16},{32,40},{40,32},{48,56},{56,48},{64,72... | collective-permute-start | bytes 491528 | tf_op jit(solution)/shard_map/ppermute | solution.py:256
  66.2 0.9 %shard_map.65 = bf16[2,4,64,256]{3,2,1,0:T(8,128)(2,1)} custom-call(s32[2,3]{1,0:T(2,128)S(1)} %get-tuple-element.9.picks, s16[8,56,256]{2,1,0:T(8,128)(2,1)S(1)} %all_to_all.17.final.own), custom_call_target="tpu_custom_call" | custom-call | tf_op jit(solution)/shard_map/pallas_call | solution.py:257
  67.1 0.1 collective-permute-done.3.other
  67.3 0.0 copy-done
  67.3 1.0 %shard_map.66 = f32[2,256,256]{2,1,0:T(8,128)} custom-call(s16[8,56,256]{2,1,0:T(8,128)(2,1)S(1)} %all_to_all.17.final.own, s16[8,40,256]{2,1,0:T(8,128)(2,1)S(1)} %collective-permute-done.3.other, f32[2,256,256]{2,1,0:T(8,128)S(1)} %copy-done), custom_call_target="tpu_custom_call" | custom-call | tf_op jit(solution)/shard_map/pallas_call | solution.py:260
  (1 shorter events, 0.0 us)
Async XLA Ops:
  2.8 13.2 %collective-permute-start = (bf16[2,512,256]{2,1,0:T(8,128)(2,1)S(1)}, bf16[2,512,256]{2,1,0:T(8,128)(2,1)S(1)}, u32[]{:S(2)}, u32[]{:S(2)}) collective-permute-start(bf16[2,512,256]{2,1,0:T(8,128)(2,1)S(1)} %get-tuple-element.10.chosen), channel_id=1, source_target_pairs={{0,64},{1,0},{2,32},{3,96},{4,80},{5,16},{6,48},{7,112},{8,97},{9,... | collective-permute-start | bytes 1572872 | tf_op jit(solution)/shard_map/ppermute | solution.py:221
  16.0 1.9 %collective-permute-start.1 = (bf16[2,512,256]{2,1,0:T(8,128)(2,1)S(1)}, bf16[2,512,256]{2,1,0:T(8,128)(2,1)S(1)}, u32[]{:S(2)}, u32[]{:S(2)}) collective-permute-start(bf16[2,512,256]{2,1,0:T(8,128)(2,1)S(1)} %collective-permute-done.own), channel_id=1, source_target_pairs={{0,8},{8,0},{16,24},{24,16},{32,40},{40,32},{48,56},{56,48},{64,72... | collective-permute-start | bytes 1572872 | tf_op jit(solution)/shard_map/ppermute | solution.py:236
  18.8 48.4 %copy-start = (f32[2,256,256]{2,1,0:T(8,128)S(1)}, f32[2,256,256]{2,1,0:T(8,128)}, u32[]{:S(2)}) copy-start(f32[2,256,256]{2,1,0:T(8,128)} %diag_inverse.1) | copy-start | bytes 1572868
  39.2 2.0 %collective-permute-start.2 = (f32[2,16,256]{2,1,0:T(8,128)S(1)}, f32[2,16,256]{2,1,0:T(8,128)S(1)}, u32[]{:S(2)}, u32[]{:S(2)}) collective-permute-start(f32[2,16,256]{2,1,0:T(8,128)S(1)} %get-tuple-element.14), channel_id=1, source_target_pairs={{0,8},{8,0},{16,24},{24,16},{32,40},{40,32},{48,56},{56,48},{64,72... | collective-permute-start | bytes 98312 | tf_op jit(solution)/shard_map/ppermute | solution.py:251
  63.5 3.7 %collective-permute-start.3 = (s16[8,40,256]{2,1,0:T(8,128)(2,1)S(1)}, s16[8,40,256]{2,1,0:T(8,128)(2,1)S(1)}, u32[]{:S(2)}, u32[]{:S(2)}) collective-permute-start(s16[8,40,256]{2,1,0:T(8,128)(2,1)S(1)} %slice.4), channel_id=1, source_target_pairs={{0,8},{8,0},{16,24},{24,16},{32,40},{40,32},{48,56},{56,48},{64,72... | collective-permute-start | bytes 491528 | tf_op jit(solution)/shard_map/ppermute | solution.py:256
